TPU v7x, 32 devices: a whole 2x2x4 slice. The times are simulated.
32 devices in a mesh: dp: 8 (over y, x, core), seq: 4 (over z).
Axes of the slice: x: 2, y: 2, z: 4, core: 2. Of those that a mesh axis runs over, the one named last changes fastest.
Arguments:
- tokens: bfloat16 [16, 1024, 768], P('dp', 'seq'), may hold values from -6 to 6
- chars: bfloat16 [16, 1024, 4, 768], P('dp', 'seq'), may hold values from -6 to 6
- char_counts: int32 [16, 1024], P('dp', 'seq'), may hold values from 1 to 4
- lengths: int32 [16], replicated, may hold values from 128 to 1024, as said below
- perm: int32 [2, 8], replicated, may hold values from 0 to 7, as said below
- token_out_cotangent: bfloat16 [16, 1024, 768], P('dp', 'seq'), may hold values from -6 to 6
- char_out_cotangent: bfloat16 [16, 1024, 768], P('dp', 'seq'), may hold values from -6 to 6
- w_qkv: float32 [768, 2304], P('dp'), may hold values from -0.21875 to 0.21875
- b_qv: float32 [1536], P('dp'), may hold values from -1.75 to 1.75
- w_out: float32 [768, 768], P('dp'), may hold values from -0.875 to 0.875
- w_in: float32 [768, 3072], P('dp'), may hold values from -0.21875 to 0.21875
- b_in: float32 [3072], P('dp'), may hold values from -1.75 to 1.75
- w_back: float32 [3072, 768], P('dp'), may hold values from -0.109375 to 0.109375
- gru_x: float32 [768, 2304], P('dp'), may hold values from -0.21875 to 0.21875
- gru_h: float32 [384, 2304], P('dp'), may hold values from -0.3125 to 0.3125
- gru_bias: float32 [2304, 2], P('dp'), may hold values from -1.75 to 1.75
- blend_w: float32 [768, 1536], P('dp'), may hold values from -0.21875 to 0.21875
- conv_w: float32 [4608, 1536], P('dp'), may hold values from -0.09375 to 0.09375
- conv_b: float32 [1536], P('dp'), may hold values from -1.75 to 1.75
- norm_gain: float32 [768, 4], P('dp'), may hold values from 0.1 to 1.9
- norm_bias: float32 [768, 4], P('dp'), may hold values from -1.75 to 1.75
- row_bias: float32 [768, 4], P('dp'), may hold values from -1.75 to 1.75
Outputs:
- token_out: bfloat16 [16, 1024, 768], P('dp', 'seq')
- char_out: bfloat16 [16, 1024, 768], P('dp', 'seq')
- tokens_grad: bfloat16 [16, 1024, 768], P('dp', 'seq')
- chars_grad: bfloat16 [16, 1024, 4, 768], P('dp', 'seq')
- w_qkv_grad: float32 [768, 2304], P('dp')
- b_qv_grad: float32 [1536], P('dp')
- w_out_grad: float32 [768, 768], P('dp')
- w_in_grad: float32 [768, 3072], P('dp')
- b_in_grad: float32 [3072], P('dp')
- w_back_grad: float32 [3072, 768], P('dp')
- gru_x_grad: float32 [768, 2304], P('dp')
- gru_h_grad: float32 [384, 2304], P('dp')
- gru_bias_grad: float32 [2304, 2], P('dp')
- blend_w_grad: float32 [768, 1536], P('dp')
- conv_w_grad: float32 [4608, 1536], P('dp')
- conv_b_grad: float32 [1536], P('dp')
- norm_gain_grad: float32 [768, 4], P('dp')
- norm_bias_grad: float32 [768, 4], P('dp')
- row_bias_grad: float32 [768, 4], P('dp')
Inputs may be any that keep to these rules, and one draw needn't show every extreme that they name: Positions j < lengths[s] of sequence s are valid keys; the first sequence is full and the second has exactly 128 valid positions. perm[m, g] is g xor perm[m, 0] (bitwise) for every group g; perm[m, 0] is never 0, and differs from one micro-batch to another. `char_counts`: characters of each token; its other rows of chars are unused.
All inputs are finite; a program needn't handle non-finite values.
Results may differ from a plain program's by a relative error of at most 0.019.
The roundings to bfloat16 on the way count: a program that leaves them out, or rounds other values in their place, can miss the bound.
Values may be sent and summed in bfloat16 or wider, within the bound.
A program may use at most 384 MiB of HBM per device.

v0:
```python
from functools import partial

import jax
import jax.numpy as jnp
from jax import lax
from jax.experimental import pallas as pl
from jax.experimental.pallas import tpu as pltpu
from jax.sharding import PartitionSpec as P

HEAD = 64
H = 384
NCHAR = 4
WIDE = 768
BF = jnp.bfloat16
F32 = jnp.float32


def dot_plain(left, right):
    return jnp.dot(left, right, preferred_element_type=F32)


def dot_left(left, right):
    return lax.dot_general(left, right, (((0,), (0,)), ((), ())), preferred_element_type=F32)


def dot_right(left, right):
    return lax.dot_general(left, right, (((1,), (1,)), ((), ())), preferred_element_type=F32)


def column_sum(values):
    return jnp.sum(values.astype(F32), axis=0)


def norm_rows(values, gain, shift):
    center = values - jnp.mean(values, axis=-1, keepdims=True)
    spread = jnp.mean(center * center, axis=-1, keepdims=True)
    rstd = lax.rsqrt(spread + 1e-06)
    return center * rstd * gain + shift


def norm_back(values, gain, grad):
    center = values - jnp.mean(values, axis=-1, keepdims=True)
    spread = jnp.mean(center * center, axis=-1, keepdims=True)
    rstd = lax.rsqrt(spread + 1e-06)
    hat = center * rstd
    lead = grad * gain
    back = rstd * (
        lead
        - jnp.mean(lead, axis=-1, keepdims=True)
        - hat * jnp.mean(lead * hat, axis=-1, keepdims=True)
    )
    return back, jnp.sum(grad * hat, axis=0), jnp.sum(grad, axis=0)


def gelu_both(values):
    cdf = 0.5 * (1.0 + lax.erf(values * (0.5**0.5)))
    pdf = jnp.exp(-0.5 * values * values) * 0.3989422804014327
    return values * cdf, cdf + values * pdf


def gru_order(side):
    return range(NCHAR) if side == 0 else range(NCHAR - 1, -1, -1)


def gru_cell(live, gates, recur, state):
    width = state.shape[-1]
    reset = jax.nn.sigmoid(gates[:, :width] + recur[:, :width])
    update = jax.nn.sigmoid(gates[:, width : 2 * width] + recur[:, width : 2 * width])
    fresh = jnp.tanh(gates[:, 2 * width :] + reset * recur[:, 2 * width :])
    after = jnp.where(live, (1.0 - update) * fresh + update * state, state)
    return reset, update, fresh, after


def gru_forward_kernel(count_ref, chars_ref, x_ref, h_ref, bias_ref, out_ref, gate_ref):
    rows = chars_ref.shape[1]
    three = 3 * H
    counts = jnp.broadcast_to(count_ref[...], (rows, H))
    chars = chars_ref[...].reshape(NCHAR * rows, chars_ref.shape[2])
    for side in range(2):
        columns = slice(side * three, (side + 1) * three)
        gate_ref[...] = dot_plain(chars, x_ref[:, columns]) + bias_ref[0:1, columns]
        state = jnp.zeros((rows, H), F32)
        for position in gru_order(side):
            recur = dot_plain(state.astype(BF), h_ref[:, columns]) + bias_ref[1:2, columns]
            gates = gate_ref[position * rows : (position + 1) * rows, :]
            state = gru_cell(position < counts, gates, recur, state)[3]
        out_ref[:, side * H : (side + 1) * H] = state


def gru_specs(high, width):
    three = 3 * H
    return [
        pl.BlockSpec((high, 1), lambda i: (i, 0)),
        pl.BlockSpec((NCHAR, high, width), lambda i: (0, i, 0)),
        pl.BlockSpec((width, 2 * three), lambda i: (0, 0)),
        pl.BlockSpec((H, 2 * three), lambda i: (0, 0)),
        pl.BlockSpec((2, 2 * three), lambda i: (0, 0)),
    ]


def gru_forward(counts, chars, gru_x, gru_h, gru_bias, high=256):
    rows, width = chars.shape[1:]
    products = NCHAR * rows * (width + H) * 6 * H
    return pl.pallas_call(
        gru_forward_kernel,
        grid=(rows // high,),
        in_specs=gru_specs(high, width),
        out_specs=pl.BlockSpec((high, 2 * H), lambda i: (i, 0)),
        out_shape=jax.ShapeDtypeStruct((rows, 2 * H), F32),
        scratch_shapes=[pltpu.VMEM((NCHAR * high, 3 * H), F32)],
        cost_estimate=pl.CostEstimate(
            flops=2 * products, bytes_accessed=10_000_000, transcendentals=24 * rows * H
        ),
        name="gru_forward",
    )(counts, chars, gru_x, gru_h, gru_bias)


def gru_backward_kernel(
    count_ref,
    chars_ref,
    x_ref,
    h_ref,
    bias_ref,
    grad_ref,
    gates_out,
    h_out,
    bias_out,
    gate_ref,
    keep_ref,
    state_ref,
    low_ref,
    recur_ref,
    total_ref,
):
    rows = chars_ref.shape[1]
    three = 3 * H
    counts = jnp.broadcast_to(count_ref[...], (rows, H))
    chars = chars_ref[...].reshape(NCHAR * rows, chars_ref.shape[2])

    @pl.when(pl.program_id(0) == 0)
    def _():
        bias_out[...] = jnp.zeros_like(bias_out)
        total_ref[...] = jnp.zeros_like(total_ref)

    for side in range(2):
        columns = slice(side * three, (side + 1) * three)
        gate_ref[...] = dot_plain(chars, x_ref[:, columns]) + bias_ref[0:1, columns]
        state = jnp.zeros((rows, H), F32)
        for position in gru_order(side):
            part = slice(position * rows, (position + 1) * rows)
            low = state.astype(BF)
            low_ref[part, :] = low
            state_ref[part, :] = state
            recur = dot_plain(low, h_ref[:, columns]) + bias_ref[1:2, columns]
            keep_ref[part, :] = recur[:, 2 * H :]
            reset, update, fresh, state = gru_cell(
                position < counts, gate_ref[part, :], recur, state
            )
            gate_ref[part, :H] = reset
            gate_ref[part, H : 2 * H] = update
            gate_ref[part, 2 * H :] = fresh
        grad = grad_ref[:, side * H : (side + 1) * H]
        gate_sum = jnp.zeros((1, three), F32)
        recur_sum = jnp.zeros((1, three), F32)
        for position in reversed(gru_order(side)):
            part = slice(position * rows, (position + 1) * rows)
            live = position < counts
            reset = gate_ref[part, :H]
            update = gate_ref[part, H : 2 * H]
            fresh = gate_ref[part, 2 * H :]
            moved = jnp.where(live, grad, 0.0)
            d_fresh = moved * (1.0 - update) * (1.0 - fresh * fresh)
            d_update = moved * (state_ref[part, :] - fresh) * update * (1.0 - update)
            d_reset = d_fresh * keep_ref[part, :] * reset * (1.0 - reset)
            d_gate = jnp.concatenate([d_reset, d_update, d_fresh], axis=-1).astype(BF)
            d_recur = jnp.concatenate([d_reset, d_update, d_fresh * reset], axis=-1).astype(BF)
            gates_out[position, :, columns] = d_gate
            recur_ref[part, :] = d_recur
            gate_sum += jnp.sum(d_gate.astype(F32), axis=0, keepdims=True)
            recur_sum += jnp.sum(d_recur.astype(F32), axis=0, keepdims=True)
            grad = jnp.where(live, moved * update, grad) + dot_right(d_recur, h_ref[:, columns])
        bias_out[0:1, columns] += gate_sum
        bias_out[1:2, columns] += recur_sum
        total_ref[:, columns] += dot_left(low_ref[...], recur_ref[...])

    @pl.when(pl.program_id(0) == pl.num_programs(0) - 1)
    def _():
        h_out[...] = total_ref[...].astype(BF)


def gru_backward(counts, chars, gru_x, gru_h, gru_bias, grad, high=256):
    rows, width = chars.shape[1:]
    three = 3 * H
    products = NCHAR * rows * (width + 3 * H) * 6 * H
    return pl.pallas_call(
        gru_backward_kernel,
        grid=(rows // high,),
        in_specs=gru_specs(high, width) + [pl.BlockSpec((high, 2 * H), lambda i: (i, 0))],
        out_specs=[
            pl.BlockSpec((NCHAR, high, 2 * three), lambda i: (0, i, 0)),
            pl.BlockSpec((H, 2 * three), lambda i: (0, 0)),
            pl.BlockSpec((2, 2 * three), lambda i: (0, 0)),
        ],
        out_shape=[
            jax.ShapeDtypeStruct((NCHAR, rows, 2 * three), BF),
            jax.ShapeDtypeStruct((H, 2 * three), BF),
            jax.ShapeDtypeStruct((2, 2 * three), F32),
        ],
        scratch_shapes=[
            pltpu.VMEM((NCHAR * high, three), F32),
            pltpu.VMEM((NCHAR * high, H), F32),
            pltpu.VMEM((NCHAR * high, H), F32),
            pltpu.VMEM((NCHAR * high, H), BF),
            pltpu.VMEM((NCHAR * high, three), BF),
            pltpu.VMEM((H, 2 * three), F32),
        ],
        cost_estimate=pl.CostEstimate(
            flops=2 * products, bytes_accessed=30_000_000, transcendentals=24 * rows * H
        ),
        name="gru_backward",
    )(counts, chars, gru_x, gru_h, gru_bias, grad)


def attention_forward_kernel(per, len_ref, qkv_ref, out_ref):
    block = pl.program_id(1)
    length = len_ref[pl.program_id(0)]
    span = per * HEAD
    total = qkv_ref.shape[0] * qkv_ref.shape[2]
    rows = qkv_ref.shape[2]
    q_all = qkv_ref[block, 0, :, :span] * BF(HEAD ** (-0.5))
    k_all = qkv_ref[:, 0, :, span : 2 * span].reshape(total, span)
    v_all = qkv_ref[:, 0, :, 2 * span :].reshape(total, span)
    valid = lax.broadcasted_iota(jnp.int32, (rows, total), 1) < length
    pieces = []
    for j in range(per):
        part = slice(j * HEAD, (j + 1) * HEAD)
        scores = jnp.where(valid, dot_right(q_all[:, part], k_all[:, part]), -1e30)
        raised = jnp.exp(scores - jnp.max(scores, axis=-1, keepdims=True))
        share = 1.0 / jnp.sum(raised, axis=-1, keepdims=True)
        probs = (raised * share).astype(BF)
        pieces.append(dot_plain(probs, v_all[:, part]))
    out_ref[0, 0] = jnp.concatenate(pieces, axis=-1).astype(BF)


def attention_forward(qkv, lengths, per):
    seqs, rows = qkv.shape[1], qkv.shape[2]
    parts = qkv.shape[0]
    span = per * HEAD
    return pl.pallas_call(
        partial(attention_forward_kernel, per),
        grid_spec=pltpu.PrefetchScalarGridSpec(
            num_scalar_prefetch=1,
            grid=(seqs, parts),
            in_specs=[pl.BlockSpec((parts, 1, rows, 3 * span), lambda m, b, n: (0, m, 0, 0))],
            out_specs=pl.BlockSpec((1, 1, rows, span), lambda m, b, n: (b, m, 0, 0)),
        ),
        out_shape=jax.ShapeDtypeStruct((parts, seqs, rows, span), BF),
        name="attend_forward",
    )(lengths, qkv)


def attention_backward_kernel(per, len_ref, qkv_ref, grad_ref, out_ref, key_acc, value_acc):
    block = pl.program_id(1)
    length = len_ref[pl.program_id(0)]
    span = per * HEAD
    parts, rows = qkv_ref.shape[0], qkv_ref.shape[2]
    total = parts * rows
    scale = HEAD ** (-0.5)

    @pl.when(block == 0)
    def _():
        key_acc[...] = jnp.zeros_like(key_acc)
        value_acc[...] = jnp.zeros_like(value_acc)

    q_all = qkv_ref[block, 0, :, :span] * BF(scale)
    g_all = grad_ref[block, 0]
    k_all = qkv_ref[:, 0, :, span : 2 * span].reshape(total, span)
    v_all = qkv_ref[:, 0, :, 2 * span :].reshape(total, span)
    valid = lax.broadcasted_iota(jnp.int32, (total, rows), 0) < length
    q_pieces, k_pieces, v_pieces = [], [], []
    for j in range(per):
        part = slice(j * HEAD, (j + 1) * HEAD)
        q, g, k, v = q_all[:, part], g_all[:, part], k_all[:, part], v_all[:, part]
        scores = jnp.where(valid, dot_right(k, q), -1e30)
        raised = jnp.exp(scores - jnp.max(scores, axis=0, keepdims=True))
        probs = raised * (1.0 / jnp.sum(raised, axis=0, keepdims=True))
        d_probs = dot_right(v, g)
        delta = jnp.sum(d_probs * probs, axis=0, keepdims=True)
        d_scores = (probs * (d_probs - delta)).astype(BF)
        q_pieces.append(dot_left(d_scores, k) * scale)
        k_pieces.append(dot_plain(d_scores, q))
        v_pieces.append(dot_plain(probs.astype(BF), g))
    out_ref[block, 0, :, :span] = jnp.concatenate(q_pieces, axis=-1).astype(BF)
    key_acc[...] += jnp.concatenate(k_pieces, axis=-1)
    value_acc[...] += jnp.concatenate(v_pieces, axis=-1)

    @pl.when(block == parts - 1)
    def _():
        out_ref[:, 0, :, span : 2 * span] = key_acc[...].astype(BF).reshape(parts, rows, span)
        out_ref[:, 0, :, 2 * span :] = value_acc[...].astype(BF).reshape(parts, rows, span)


def attention_backward(qkv, grads, lengths, per):
    parts, seqs, rows, _ = qkv.shape
    span = per * HEAD
    return pl.pallas_call(
        partial(attention_backward_kernel, per),
        grid_spec=pltpu.PrefetchScalarGridSpec(
            num_scalar_prefetch=1,
            grid=(seqs, parts),
            in_specs=[
                pl.BlockSpec((parts, 1, rows, 3 * span), lambda m, b, n: (0, m, 0, 0)),
                pl.BlockSpec((parts, 1, rows, span), lambda m, b, n: (0, m, 0, 0)),
            ],
            out_specs=pl.BlockSpec((parts, 1, rows, 3 * span), lambda m, b, n: (0, m, 0, 0)),
            scratch_shapes=[
                pltpu.VMEM((parts * rows, span), F32),
                pltpu.VMEM((parts * rows, span), F32),
            ],
        ),
        out_shape=jax.ShapeDtypeStruct(qkv.shape, BF),
        name="attend_backward",
    )(lengths, qkv, grads)


def exchange(blocks):
    return lax.all_to_all(blocks, "seq", split_axis=0, concat_axis=0)


def relocate_begin(pair, step):
    count = lax.axis_size("dp")
    levels = count.bit_length() - 1
    bits = (step, step if step == 0 else levels - step)
    others = []
    for value, bit in zip(pair, bits):
        apart = 1 << bit
        pairs = [(source, source ^ apart) for source in range(count)]
        others.append(lax.ppermute(value, "dp", pairs))
    return bits, tuple(others)


def relocate_end(masks, pair, begun):
    done = []
    for value, bit, other in zip(pair, *begun):
        moving = (jnp.bitwise_and(masks, 1 << bit) != 0)[:, None, None]
        done.append(jnp.where(moving, other, value))
    return tuple(done)


def relocate_one(masks, pair, step, tie):
    bits, others = relocate_begin(pair, step)
    others, pair, tie = lax.optimization_barrier((others, pair, tie))
    return relocate_end(masks, pair, (bits, others)), tie


def relocate_last(masks, pair, first, tie):
    levels = lax.axis_size("dp").bit_length() - 1
    for step in range(first, levels):
        bits, others = relocate_begin(pair, step)
        if step == levels - 1:
            others, pair, _ = lax.optimization_barrier((others, pair, tie))
        pair = relocate_end(masks, pair, (bits, others))
    return pair


def edges(block):
    count = lax.axis_size("seq")
    forward = [(i, i + 1) for i in range(count - 1)]
    backward = [(target, source) for source, target in forward]
    low = lax.ppermute(block[:, -1:], "seq", forward)
    high = lax.ppermute(block[:, :1], "seq", backward)
    return low, high


LINE = ([(0, 1), (3, 2)], [(1, 2), (2, 1)], [(1, 0), (2, 3)])


def line_sum(value, step):
    if lax.axis_size("seq") != 4:
        return lax.psum(value, "seq") if step == 0 else value
    other = lax.ppermute(value, "seq", LINE[step])
    if step < 2:
        return value + other
    return jnp.where((lax.axis_index("seq") % 3) == 0, other, value)


def shifted(block, low, high):
    before = jnp.concatenate([low, block[:, :-1]], axis=1)
    after = jnp.concatenate([block[:, 1:], high], axis=1)
    flat = (-1, block.shape[-1])
    return before.reshape(flat), block.reshape(flat), after.reshape(flat)


def sum_plan(shapes, high):
    spans, start = [], 0
    for rows, columns in shapes:
        tall = rows // high
        count = tall * (columns // WIDE)
        spans.append((start, start + count, tall))
        start += count
    return spans, start


def sum_kernel(spans, pre_spans, late, pre, high, lag, slots, *refs):
    whole = len(spans)
    count = whole + len(pre_spans)
    total = late + pre
    ins, outs = refs[:count], refs[count : 2 * count]
    own, rc, sc, s1a, s1b, r1a, r1b, r2a, r2b, s2, rz, sz, rm, tot, ready = refs[
        2 * count : 2 * count + 15
    ]
    sems = refs[2 * count + 15]
    credits = refs[2 * count + 16]
    half = WIDE // 2
    dp, z = lax.axis_index("dp"), lax.axis_index("seq")
    core, x, y = dp % 2, (dp // 2) % 2, dp // 4
    at_core = {"dp": dp + 1 - 2 * core}
    at_x = {"dp": dp + 2 - 4 * x}
    at_y = {"dp": dp + 4 - 8 * y}
    outer = (z % 3) == 0
    inner = (z % 3) != 0
    at_inner = {"seq": 1 + z // 3}
    at_middle = {"seq": (3 - z) % 4}
    at_outer = {"seq": (z // 2) * 3}

    barrier = pltpu.get_barrier_semaphore()

    def greet(where):
        pl.semaphore_signal(barrier, inc=1, device_id=where, device_id_type=pl.DeviceIdType.MESH)

    greet(at_core)
    greet(at_x)
    greet(at_y)

    @pl.when(outer)
    def _():
        greet(at_inner)
        pl.semaphore_wait(barrier, 4)

    @pl.when(inner)
    def _():
        greet(at_middle)
        greet(at_outer)
        pl.semaphore_wait(barrier, 5)

    def remote(source, target, name, slot, where):
        return pltpu.make_async_remote_copy(
            src_ref=source,
            dst_ref=target,
            send_sem=sems.at[2 * name, slot],
            recv_sem=sems.at[2 * name + 1, slot],
            device_id=where,
            device_id_type=pl.DeviceIdType.MESH,
        )

    CORE, X1, Y1, X2, Y2, OUTER, MIDDLE, FINAL, LOCAL, READY = range(10)

    def give_credit(name, k, where):
        @pl.when(k + slots < total)
        def _():
            pl.semaphore_signal(
                credits.at[name], inc=1, device_id=where, device_id_type=pl.DeviceIdType.MESH
            )

    def take_credit(name, k):
        @pl.when(k >= slots)
        def _():
            pl.semaphore_wait(credits.at[name], 1)

    def send_core(slot, source):
        return remote(source, rc.at[slot], CORE, slot, at_core)

    def send_x1(slot):
        return remote(sc.at[slot, :, 1 - x, :, :half], r1a.at[slot], X1, slot, at_x)

    def send_y1(slot):
        return remote(sc.at[slot, 1 - y, :, :, half:], r1b.at[slot], Y1, slot, at_y)

    def send_y2(slot):
        return remote(s1a.at[slot, 1 - y], r2a.at[slot], Y2, slot, at_y)

    def send_x2(slot):
        return remote(s1b.at[slot, 1 - x], r2b.at[slot], X2, slot, at_x)

    def send_outer(slot):
        return remote(s2.at[slot], rz.at[slot], OUTER, slot, at_inner)

    def send_middle(slot):
        return remote(sz.at[slot], rm.at[slot], MIDDLE, slot, at_middle)

    def send_final(slot, target):
        return remote(tot.at[slot], target, FINAL, slot, at_outer)

    def load(slot, source):
        return pltpu.make_async_copy(source, own.at[slot], sems.at[2 * LOCAL, slot])

    def load_ready(slot, source):
        return pltpu.make_async_copy(source, ready.at[slot], sems.at[2 * READY, slot])

    def save(slot, target):
        return pltpu.make_async_copy(tot.at[slot], target, sems.at[2 * LOCAL + 1, slot])

    def window(ref, j, tall):
        return pl.ds((j % tall) * high, high), pl.ds((j // tall) * WIDE, WIDE)

    def is_pre(k):
        return (k < 3 * pre) & (k % 3 == 2)

    def late_index(k):
        return jnp.where(k < 3 * pre, (k // 3) * 2 + k % 3, k - pre)

    def each(k, plan, parts, index, run):
        for (start, stop, tall), ref in zip(plan, parts):

            @pl.when((index >= start) & (index < stop))
            def _():
                run(ref, *window(ref, index - start, tall))

    def on_late(k, run):
        pl.when(jnp.logical_not(is_pre(k)))(run)

    def on_pre(k, run):
        pl.when(is_pre(k))(run)

    def add(left, right):
        return (left.astype(F32) + right.astype(F32)).astype(BF)

    def stage(k, run):
        @pl.when((k >= 0) & (k < total))
        def _():
            run(k, lax.rem(jnp.maximum(k, 0), slots))

    first = ins[0].at[:, core, pl.ds(0, high), pl.ds(0, WIDE)]
    final = outs[0].at[pl.ds(0, high), pl.ds(0, WIDE)]
    early = ins[whole].at[pl.ds(0, high), pl.ds(0, WIDE)]

    @pl.loop(0, total + 6 * lag)
    def _(t):
        def begin(k, slot):
            take_credit(CORE, k)

            def go():
                def run(ref, rows, columns):
                    send_core(slot, ref.at[:, 1 - core, rows, columns]).start()
                    load(slot, ref.at[:, core, rows, columns]).start()

                each(k, spans, ins[:whole], late_index(k), run)

            on_late(k, go)

        def add_core(k, slot):
            def go():
                load(slot, first).wait()
                send_core(slot, first).wait()
                both = add(own[slot], rc[slot])
                sc[slot] = both.reshape(2, 2, high, WIDE)

            on_late(k, go)
            give_credit(CORE, k, at_core)

        def add_one(k, slot):
            def go():
                send_x1(slot).wait()
                send_y1(slot).wait()
                s1a[slot] = add(sc[slot, :, x, :, :half], r1a[slot])
                s1b[slot] = add(sc[slot, y, :, :, half:], r1b[slot])

            on_late(k, go)
            give_credit(X1, k, at_x)
            give_credit(Y1, k, at_y)

        def add_two(k, slot):
            def go():
                send_y2(slot).wait()
                send_x2(slot).wait()
                s2[slot, :, :half] = add(s1a[slot, y], r2a[slot])
                s2[slot, :, half:] = add(s1b[slot, x], r2b[slot])

            def take():
                load_ready(slot, early).wait()
                s2[slot] = ready[slot]

            on_late(k, go)
            on_pre(k, take)
            give_credit(Y2, k, at_y)
            give_credit(X2, k, at_x)

        def add_outer(k, slot):
            @pl.when(outer)
            def _():
                send_outer(slot).wait_send()

            @pl.when(inner)
            def _():
                send_outer(slot).wait_recv()
                sz[slot] = add(s2[slot], rz[slot])
                give_credit(OUTER, k, at_outer)

        def add_middle(k, slot):
            @pl.when(inner)
            def _():
                send_middle(slot).wait()
                tot[slot] = add(sz[slot], rm[slot])
                give_credit(MIDDLE, k, at_middle)

        def finish(k, slot):
            @pl.when(inner)
            def _():
                save(slot, final).wait()
                send_final(slot, final).wait_send()

            @pl.when(outer)
            def _():
                send_final(slot, final).wait_recv()
                give_credit(FINAL, k, at_inner)

        def go_one(k, slot):
            take_credit(X1, k)
            take_credit(Y1, k)

            def go():
                send_x1(slot).start()
                send_y1(slot).start()

            on_late(k, go)

        def go_two(k, slot):
            take_credit(Y2, k)
            take_credit(X2, k)

            def go():
                send_y2(slot).start()
                send_x2(slot).start()

            def fetch():
                def run(ref, rows, columns):
                    load_ready(slot, ref.at[rows, columns]).start()

                each(k, pre_spans, ins[whole:], k // 3, run)

            on_late(k, go)
            on_pre(k, fetch)

        def go_outer(k, slot):
            @pl.when(outer)
            def _():
                take_credit(OUTER, k)
                send_outer(slot).start()

        def go_middle(k, slot):
            @pl.when(inner)
            def _():
                take_credit(MIDDLE, k)
                send_middle(slot).start()

        def go_final(k, slot):
            @pl.when(inner)
            def _():
                take_credit(FINAL, k)

                def run(ref, rows, columns):
                    save(slot, ref.at[rows, columns]).start()
                    send_final(slot, ref.at[rows, columns]).start()

                on_late(k, lambda: each(k, spans, outs[:whole], late_index(k), run))
                on_pre(k, lambda: each(k, pre_spans, outs[whole:], k // 3, run))

        stage(t, begin)
        stage(t - lag, add_core)
        stage(t - 2 * lag, add_one)
        stage(t - 3 * lag, add_two)
        stage(t - 4 * lag, add_outer)
        stage(t - 5 * lag, add_middle)
        stage(t - lag, go_one)
        stage(t - 2 * lag, go_two)
        stage(t - 3 * lag, go_outer)
        stage(t - 4 * lag, go_middle)
        stage(t - 5 * lag, go_final)
        stage(t - 6 * lag, finish)


def sum_grads(grads, pres, high=48, lag=3, slots=6):
    shapes = [(grad.shape[0] // 8, grad.shape[1]) for grad in grads]
    pre_shapes = [grad.shape for grad in pres]
    spans, late = sum_plan(shapes, high)
    pre_spans, pre = sum_plan(pre_shapes, high)
    half = WIDE // 2
    anywhere = pl.BlockSpec(memory_space=pl.ANY)
    blocks = [grad.reshape(4, 2, grad.shape[0] // 8, grad.shape[1]) for grad in grads]
    shapes = shapes + pre_shapes
    return pl.pallas_call(
        partial(sum_kernel, spans, pre_spans, late, pre, high, lag, slots),
        in_specs=[anywhere] * len(shapes),
        out_specs=[anywhere] * len(shapes),
        out_shape=[jax.ShapeDtypeStruct(shape, BF) for shape in shapes],
        scratch_shapes=[
            pltpu.VMEM((slots, 4, high, WIDE), BF),
            pltpu.VMEM((slots, 4, high, WIDE), BF),
            pltpu.VMEM((slots, 2, 2, high, WIDE), BF),
            pltpu.VMEM((slots, 2, high, half), BF),
            pltpu.VMEM((slots, 2, high, half), BF),
            pltpu.VMEM((slots, 2, high, half), BF),
            pltpu.VMEM((slots, 2, high, half), BF),
            pltpu.VMEM((slots, high, half), BF),
            pltpu.VMEM((slots, high, half), BF),
            pltpu.VMEM((slots, high, WIDE), BF),
            pltpu.VMEM((slots, high, WIDE), BF),
            pltpu.VMEM((slots, high, WIDE), BF),
            pltpu.VMEM((slots, high, WIDE), BF),
            pltpu.VMEM((slots, high, WIDE), BF),
            pltpu.VMEM((slots, high, WIDE), BF),
            pltpu.SemaphoreType.DMA((20, slots)),
            pltpu.SemaphoreType.REGULAR((8,)),
        ],
        compiler_params=pltpu.CompilerParams(collective_id=1, has_side_effects=True),
        name="sum_grads",
    )(*blocks, *pres)


def heads_first(weight, parts):
    rows = weight.shape[0]
    split = weight.reshape(rows, 3, parts, WIDE // parts)
    return split.transpose(0, 2, 1, 3).reshape(rows, 3 * WIDE)


def heads_last(weight, parts):
    rows = weight.shape[0]
    split = weight.reshape(rows, parts, 3, WIDE // parts)
    return split.transpose(0, 2, 1, 3).reshape(rows, 3 * WIDE)


def flat_small(small):
    return jnp.concatenate([piece.T.reshape(-1) for piece in small])


def gather_packed(weights, small, wide):
    return unpack(pack(weights, small, wide), weights, small, wide)


def pack(weights, small, wide):
    pieces = []
    for weight in weights:
        low = weight.astype(BF)
        pieces += [low[:, start : start + wide] for start in range(0, low.shape[1], wide)]
    flat = flat_small(small).astype(BF)
    high = -(-flat.size // wide)
    high = -(-high // 8) * 8
    pieces.append(jnp.pad(flat, (0, high * wide - flat.size)).reshape(high, wide))
    return lax.all_gather(jnp.concatenate(pieces, axis=0), "dp", axis=0)


def unpack(full, weights, small, wide):
    groups = full.shape[0]
    outs, at = [], 0
    for weight in weights:
        rows, columns = weight.shape
        blocks = columns // wide
        part = full[:, at : at + blocks * rows].reshape(groups, blocks, rows, wide)
        outs.append(part.transpose(0, 2, 1, 3).reshape(groups * rows, columns))
        at += blocks * rows
    used = -(-sum(piece.size for piece in small) // wide)
    table = full[:, at : at + used].astype(F32).reshape(groups, -1)
    vectors, at = [], 0
    for piece in small:
        part = table[:, at : at + piece.size]
        if piece.ndim == 2:
            rows, columns = piece.shape
            part = part.reshape(groups, columns, rows).transpose(1, 0, 2)
            vectors.append(part.reshape(columns, groups * rows))
        else:
            vectors.append(part.reshape(-1))
        at += piece.size
    return outs, vectors


def pack_small(small, groups, multiple):
    pieces = []
    for piece in small:
        columns = piece if isinstance(piece, list) else [piece]
        pieces += [column.reshape(groups, -1) for column in columns]
    flat = jnp.concatenate(pieces, axis=1)
    high = -(-flat.shape[1] // WIDE)
    high = -(-high // multiple) * multiple
    flat = jnp.pad(flat.astype(BF), ((0, 0), (0, high * WIDE - flat.shape[1])))
    return flat.reshape(groups * high, WIDE)


def sum_grads_plain(grads, pres):
    outs = [lax.psum_scatter(grad, "dp", scatter_dimension=0, tiled=True) for grad in grads]
    return [lax.psum(part, "seq") for part in outs + list(pres)]


def reduce_grads(big, pres, small):
    groups = lax.axis_size("dp")
    ours = groups == 8 and lax.axis_size("seq") == 4
    grads = [grad.astype(BF) for grad in big] + [pack_small(small, groups, 48)]
    outs = sum_grads(grads, pres) if ours else sum_grads_plain(grads, pres)
    tail = outs[len(big)]
    sizes = []
    for piece in small:
        columns = piece if isinstance(piece, list) else [piece]
        sizes.append((len(columns), columns[0].size // groups, isinstance(piece, list)))
    used = -(-sum(many * size for many, size, _ in sizes) // WIDE)
    tail = tail[:used].astype(F32).reshape(-1)
    vectors, at = [], 0
    for many, size, matrix in sizes:
        part = tail[at : at + many * size]
        vectors.append(part.reshape(many, size).T if matrix else part)
        at += many * size
    bigs = [piece.astype(F32) for piece in outs[: len(big)]]
    return bigs, [piece.astype(F32) for piece in outs[len(big) + 1 :]], vectors


def scatter_sum(grad):
    return lax.psum_scatter(grad.astype(BF), "dp", scatter_dimension=0, tiled=True)


def body(
    tokens,
    chars,
    char_counts,
    lengths,
    perm,
    token_cot,
    char_cot,
    w_qkv,
    b_qv,
    w_out,
    w_in,
    b_in,
    w_back,
    gru_x,
    gru_h,
    gru_bias,
    blend_w,
    conv_w,
    conv_b,
    norm_gain,
    norm_bias,
    row_bias,
):
    parts = lax.axis_size("seq")
    seqs, local, width = tokens.shape
    rows = seqs * local
    per = width // HEAD // parts
    three = 3 * H
    masks = perm[:, 0]
    place = lax.axis_index("dp")
    own_lengths = lax.dynamic_slice(lengths, (place * seqs,), (seqs,))
    first = (heads_first(w_qkv, parts), gru_x, gru_h)
    (w_qkv, gru_x, gru_h), (b_qv, gru_bias) = gather_packed(first, (b_qv, gru_bias), 3 * width)
    middle = (w_out, w_in, w_back, blend_w)
    small = (b_in, conv_b, norm_gain, norm_bias, row_bias)
    packed = pack(middle, small, width)
    conv_w = lax.all_gather(conv_w.astype(BF), "dp", axis=0, tiled=True)

    flat_tokens = tokens.reshape(rows, width)
    counts = char_counts.reshape(rows, 1)
    row_chars = chars.transpose(2, 0, 1, 3).reshape(NCHAR, rows, width)
    flat_chars = row_chars.reshape(NCHAR * rows, width)
    bias = jnp.concatenate([b_qv[:width], jnp.zeros((width,), F32), b_qv[width:]])
    bias = heads_first(bias[None], parts)[0]
    project = (dot_plain(flat_tokens, w_qkv) + bias).astype(BF)
    cots = (token_cot, char_cot)
    cots, project = relocate_one(masks, cots, 0, project)
    project, row_chars = lax.optimization_barrier((project, row_chars))
    span = 3 * per * HEAD
    qkv = project.reshape(seqs, local, parts, span).transpose(2, 0, 1, 3)
    qkv = exchange(qkv)
    char_state = gru_forward(counts, row_chars, gru_x, gru_h, gru_bias)
    qkv, char_state = lax.optimization_barrier((qkv, char_state))
    context = attention_forward(qkv, own_lengths, per)
    context, packed = lax.optimization_barrier((context, packed))
    middle, small = unpack(packed, middle, small, width)
    w_out, w_in, w_back, blend_w = middle
    b_in, conv_b, norm_gain, norm_bias, row_bias = small
    context = exchange(context)
    context = context.transpose(1, 2, 0, 3).reshape(rows, width)

    cots, context = relocate_one(masks, cots, 1, context)
    summed_first = flat_tokens.astype(F32) + dot_plain(context, w_out) + row_bias[0]
    hidden1 = norm_rows(summed_first, norm_gain[0], norm_bias[0])
    hidden1_low = hidden1.astype(BF)
    inner = dot_plain(hidden1_low, w_in) + b_in
    activated, inner_slope = gelu_both(inner)
    activated, inner_slope = lax.optimization_barrier((activated.astype(BF), inner_slope))
    summed_second = hidden1 + dot_plain(activated, w_back) + row_bias[1]
    hidden2 = norm_rows(summed_second, norm_gain[1], norm_bias[1])
    hidden2_low = hidden2.astype(BF)
    char_low = char_state.astype(BF)
    token_side = dot_plain(hidden2_low, blend_w[:, :width]) + row_bias[2]
    char_side = dot_plain(char_low, blend_w[:, width:]) + row_bias[3]
    joined = jnp.concatenate([token_side, char_side], axis=-1).astype(BF)
    joined = joined.reshape(seqs, local, 2 * width)
    cots, joined = lax.optimization_barrier((cots, joined))
    taps = shifted(joined, *edges(joined))
    stacked = jnp.concatenate(taps, axis=-1)
    mixed = dot_plain(stacked, conv_w) + conv_b
    lifted, mixed_slope = lax.optimization_barrier(gelu_both(mixed))
    token_pre = hidden2 + lifted[:, :width]
    char_pre = char_state + lifted[:, width:]
    token_out = norm_rows(token_pre, norm_gain[2], norm_bias[2]).astype(BF)
    char_out = norm_rows(char_pre, norm_gain[3], norm_bias[3]).astype(BF)
    outs = (token_out.reshape(seqs, local, width), char_out.reshape(seqs, local, width))
    cots = relocate_last(masks, cots, 2, (token_out, char_out))

    token_cots, char_cots = (part.reshape(rows, width).astype(F32) for part in cots)
    d_token_pre, gain_token, shift_token = norm_back(
        token_pre, norm_gain[2], token_cots
    )
    d_char_pre, gain_char, shift_char = norm_back(char_pre, norm_gain[3], char_cots)
    d_mixed = jnp.concatenate([d_token_pre, d_char_pre], axis=-1) * mixed_slope
    d_mixed = d_mixed.astype(BF)
    grad_conv = dot_left(stacked, d_mixed).astype(BF)
    grad_conv, d_mixed = lax.optimization_barrier((grad_conv, d_mixed))
    sum_conv = scatter_sum(grad_conv)
    outs, d_mixed = relocate_one(masks, outs, 0, d_mixed)
    beside = d_mixed.reshape(seqs, local, 2 * width)
    before, same, after = shifted(beside, *edges(beside))
    taps_w = conv_w.reshape(3, 2 * width, 2 * width)
    d_joined = dot_right(after, taps_w[0]) + dot_right(same, taps_w[1])
    d_joined = (d_joined + dot_right(before, taps_w[2])).astype(BF)
    d_token_side = d_joined[:, :width]
    d_char_side = d_joined[:, width:]
    grad_blend = jnp.concatenate(
        [dot_left(hidden2_low, d_token_side), dot_left(char_low, d_char_side)], axis=-1
    )
    grad_blend, d_token_side, d_char_side = lax.optimization_barrier(
        (grad_blend.astype(BF), d_token_side, d_char_side)
    )
    sum_blend = scatter_sum(grad_blend)
    d_hidden2 = d_token_pre + dot_right(d_token_side, blend_w[:, :width])
    d_char_state = d_char_pre + dot_right(d_char_side, blend_w[:, width:])

    d_second, gain_second, shift_second = norm_back(summed_second, norm_gain[1], d_hidden2)
    d_branch = d_second.astype(BF)
    grad_back = dot_left(activated, d_branch).astype(BF)
    grad_back, d_branch = lax.optimization_barrier((grad_back, d_branch))
    sum_back = scatter_sum(grad_back)
    d_inner = (dot_right(d_branch, w_back) * inner_slope).astype(BF)
    grad_in = dot_left(hidden1_low, d_inner)
    d_hidden1 = d_second + dot_right(d_inner, w_in)
    d_first, gain_first, shift_first = norm_back(summed_first, norm_gain[0], d_hidden1)
    d_attend = d_first.astype(BF)
    outs, d_attend = relocate_one(masks, outs, 1, d_attend)
    grad_out = dot_left(context, d_attend)
    d_context = dot_right(d_attend, w_out).astype(BF)
    d_context = d_context.reshape(seqs, local, parts, per * HEAD).transpose(2, 0, 1, 3)
    d_project = attention_backward(qkv, exchange(d_context), own_lengths, per)
    sum_conv, d_char_state, d_project = lax.optimization_barrier((sum_conv, d_char_state, d_project))
    d_project = exchange(d_project)
    sum_conv = line_sum(sum_conv, 0)
    d_project = d_project.transpose(1, 2, 0, 3).reshape(rows, 3 * width)

    d_gates, grad_gru_h, grad_gru_bias = gru_backward(
        counts, row_chars, gru_x, gru_h, gru_bias, d_char_state
    )
    sum_conv, d_gates = lax.optimization_barrier((sum_conv, d_gates))
    sum_conv = line_sum(sum_conv, 1)
    d_gates = d_gates.reshape(NCHAR * rows, 2 * three)
    grad_gru_x = dot_left(flat_chars, d_gates)
    chars_back = dot_right(d_gates, gru_x).astype(BF)
    chars_back, sum_conv = lax.optimization_barrier((chars_back, sum_conv))
    chars_back = chars_back.reshape(NCHAR, seqs, local, width).transpose(1, 2, 0, 3)

    grad_qkv = dot_left(flat_tokens, d_project)
    sums = heads_last(column_sum(d_project)[None], parts)[0]
    grad_b_qv = jnp.concatenate([sums[:width], sums[2 * width :]])
    tokens_back = (d_first + dot_right(d_project, w_qkv)).astype(BF)
    big = (grad_in, grad_qkv, grad_gru_x, grad_gru_h, grad_out)
    small = (
        grad_b_qv,
        column_sum(d_inner),
        [grad_gru_bias[0], grad_gru_bias[1]],
        column_sum(d_mixed),
        [gain_first, gain_second, gain_token, gain_char],
        [shift_first, shift_second, shift_token, shift_char],
        [
            column_sum(d_attend),
            column_sum(d_branch),
            column_sum(d_token_side),
            column_sum(d_char_side),
        ],
    )
    big, early, small = reduce_grads(big, (sum_back, sum_blend), small)
    outs, big[-1] = lax.optimization_barrier((outs, big[-1]))
    outs = relocate_last(masks, outs, 2, big[-1])
    g_in, g_qkv, g_gru_x, g_gru_h, g_out = big
    g_back, g_blend = early
    g_conv = line_sum(sum_conv, 2).astype(F32)
    g_b_qv, g_b_in, g_gru_bias, g_conv_b, g_gain, g_shift, g_rows = small
    return (
        outs[0],
        outs[1],
        tokens_back.reshape(seqs, local, width),
        chars_back,
        heads_last(g_qkv, parts),
        g_b_qv,
        g_out,
        g_in,
        g_b_in,
        g_back,
        g_gru_x,
        g_gru_h,
        g_gru_bias,
        g_blend,
        g_conv,
        g_conv_b,
        g_gain,
        g_shift,
        g_rows,
    )


def solution(mesh):
    rows, vector, seq = P("dp", None), P("dp"), P("dp", "seq", None)
    weights = (
        rows,
        vector,
        rows,
        rows,
        vector,
        rows,
        rows,
        rows,
        rows,
        rows,
        rows,
        vector,
        rows,
        rows,
        rows,
    )
    return jax.shard_map(
        body,
        mesh=mesh,
        in_specs=(seq, P("dp", "seq", None, None), P("dp", "seq"), P(), P(), seq, seq) + weights,
        out_specs=(seq, seq, seq, P("dp", "seq", None, None)) + weights,
        check_vma=False,
    )
```

profile of v0, /device:TPU:0, one launch (start us, length us, event | category | flops | bytes accessed | tf_op | source)
XLA Modules:
  0.0 692.3 jit_solution(2183626190527288531)
XLA Ops:
  28.1 46.2 %all-gather.8.cloned.1.call-done = bf16[1984,2304]{1,0:T(8,128)(2,1)} async-done(((bf16[248,2304]{1,0:T(8,128)(2,1)}), bf16[1984,2304]{1,0:T(8,128)(2,1)}) %all-gather.8.cloned.1.call-update) | async-done | bytes 9142288 | tf_op jit(solution)/shard_map/all_gather | solution.py:749
  75.4 5.4 fusion.68
  89.4 5.0 reshape.453
  112.0 20.1 %gru_forward.1 = f32[512,768]{1,0:T(8,128)} custom-call(s32[512,1]{1,0:T(8,128)} %bitcast.257, bf16[4,512,768]{2,1,0:T(8,128)(2,1)} %bitcast.225, bf16[768,2304]{1,0:T(8,128)(2,1)} %bitcast.220, bf16[384,2304]{1,0:T(8,128)(2,1)} %bitcast.241, f32[2,2304]{1,0:T(2,128)} %reshape.456.bias_ref), custom_call_target="tpu_custom_call" | custom-call | flops 10871635968 | bytes 10000000 | tf_op jit(solution)/shard_map/gru_forward/pallas_call | solution.py:104
  132.1 23.1 %all-to-all-done = bf16[4,2,256,576]{2,3,1,0:T(8,128)(2,1)S(1)} async-done(((bf16[4,2,256,576]{2,3,1,0:T(8,128)(2,1)}), bf16[4,2,256,576]{2,3,1,0:T(8,128)(2,1)S(1)}, u32[]{:S(2)}, u32[]{:S(2)}) %all-to-all-start) | async-done | bytes 2359328 | tf_op jit(solution)/shard_map/all_to_all | solution.py:327
  157.8 19.7 %attend_forward.1 = bf16[4,2,256,192]{3,2,1,0:T(8,128)(2,1)} custom-call(s32[2]{0:T(128)} %dynamic_slice.3.len_ref, bf16[4,2,256,576]{3,2,1,0:T(8,128)(2,1)} %copy.145.qkv_ref), custom_call_target="tpu_custom_call" | custom-call | tf_op jit(solution)/shard_map/attend_forward/pallas_call | solution.py:249
  191.0 6.7 fusion.67
  215.8 7.3 %fusion.3 = (f32[512,3072]{1,0:T(8,128)}, bf16[512,3072]{1,0:T(8,128)(2,1)S(1)}) fusion(f32[3072]{0:T(1024)S(1)} %add.232, bf16[768,3072]{1,0:T(8,128)(2,1)S(1)} %bitcast.211, f32[512,768]{1,0:T(8,128)S(1)} %get-tuple-element.236, f32[768]{0:T(1024)S(1)} %add.229, f32[768]{0:T(1024)S(1)} %mul.297, f32[512]{0:T(512)S(1)} %add_rsqrt_fusion.3, ...), kind=kOutput, calls=%fused_computation.5 | convolution fusion | flops 2435186688 | bytes 15751168 | tf_op jit(solution)/shard_map/dot_general | solution.py:19
  243.5 8.9 %all-gather.6.cloned.1.call-done = bf16[4608,1536]{1,0:T(8,128)(2,1)} async-done(((bf16[576,1536]{1,0:T(8,128)(2,1)}), bf16[4608,1536]{1,0:T(8,128)(2,1)}) %all-gather.6.cloned.1.call-update) | async-done | bytes 14155792 | tf_op jit(solution)/shard_map/all_gather | solution.py:855
  252.4 14.4 %fusion.21 = (f32[512,1536]{1,0:T(8,128)S(1)}, f32[512,1536]{1,0:T(8,128)S(1)}) fusion(f32[1536]{0:T(1024)S(1)} %add.252, bf16[4608,1536]{1,0:T(8,128)(2,1)} %all-gather.6.cloned.1.call-done, bf16[512,1536]{1,0:T(8,128)(2,1)} %bitcast.246, bf16[512,1536]{1,0:T(8,128)(2,1)S(1)} %bitcast.191, bf16[512,1536]{1,0:T(8,128)(2,1)} %bitcast.244), kind=kOutput, calls=%fused_computation.31 | convolution fusion | flops 7269777408 | bytes 25171968 | tf_op jit(solution)/shard_map/dot_general | solution.py:19
  279.7 10.9 %convolution_convert_fusion = bf16[4608,1536]{1,0:T(8,128)(2,1)} fusion(bf16[512,1536]{1,0:T(8,128)(2,1)S(1)} %fusion.22, bf16[512,1536]{1,0:T(8,128)(2,1)S(1)} %bitcast.247, bf16[512,1536]{1,0:T(8,128)(2,1)S(1)} %bitcast.192, bf16[512,1536]{1,0:T(8,128)(2,1)S(1)} %bitcast.245), kind=kOutput, calls=%fused_computation | convolution fusion | flops 7268990976 | bytes 20447232 | tf_op jit(solution)/shard_map/dot_general | solution.py:23
  306.4 5.1 fusion.6
  338.9 7.9 %fusion.80 = (bf16[3072]{0:T(1024)(128)(2,1)S(1)}, bf16[512,3072]{1,0:T(8,128)(2,1)}) fusion(f32[512,3072]{1,0:T(8,128)} %get-tuple-element.122, bf16[512,768]{1,0:T(8,128)(2,1)S(1)} %get-tuple-element.121, bf16[3072,768]{1,0:T(8,128)(2,1)} %bitcast.213), kind=kOutput, calls=%fused_computation.206 | convolution fusion | flops 2420634624 | bytes 14948352 | tf_op jit(solution)/shard_map/dot_general | solution.py:27
  346.9 7.9 %multiply_reduce_fusion.1 = (bf16[768]{0:T(1024)(128)(2,1)S(1)}, f32[512]{0:T(512)S(1)}, f32[512]{0:T(512)S(1)}, bf16[768]{0:T(1024)(128)(2,1)S(1)}, f32[512,768]{1,0:T(8,128)}) fusion(f32[512,768]{1,0:T(8,128)S(1)} %copy-done.8, f32[512]{0:T(512)S(1)} %add_rsqrt_fusion.3, f32[512]{0:T(512)S(1)} %broadcast_multiply_fusion.9, f32[768]{0:T(1024)S(1)} %mul.297, ...), kind=kOutput, calls=%fused_computation.66 | convolution fusion | flops 2419848704 | bytes 12597248 | tf_op jit(solution)/shard_map/dot_general | solution.py:27
  380.5 8.9 %all-to-all-done.2 = bf16[4,2,256,192]{2,3,1,0:T(8,128)(2,1)S(1)} async-done(((bf16[4,2,256,192]{2,3,1,0:T(8,128)(2,1)}), bf16[4,2,256,192]{2,3,1,0:T(8,128)(2,1)S(1)}, u32[]{:S(2)}, u32[]{:S(2)}) %all-to-all-start.2) | async-done | bytes 786464 | tf_op jit(solution)/shard_map/all_to_all | solution.py:327
  390.7 37.5 %attend_backward.1 = bf16[4,2,256,576]{3,2,1,0:T(8,128)(2,1)} custom-call(s32[2]{0:T(128)} %dynamic_slice.3.len_ref, bf16[4,2,256,576]{3,2,1,0:T(8,128)(2,1)} %copy.145.qkv_ref, bf16[4,2,256,192]{3,2,1,0:T(8,128)(2,1)} %copy.155.grad_ref), custom_call_target="tpu_custom_call" | custom-call | tf_op jit(solution)/shard_map/attend_backward/pallas_call | solution.py:306
  436.2 5.1 collective-permute-start.14
  441.3 36.7 %gru_backward.1 = (bf16[4,512,2304]{2,1,0:T(8,128)(2,1)}, bf16[384,2304]{1,0:T(8,128)(2,1)}, f32[2,2304]{1,0:T(2,128)}) custom-call(s32[512,1]{1,0:T(8,128)} %bitcast.258, bf16[4,512,768]{2,1,0:T(8,128)(2,1)} %bitcast.226, bf16[768,2304]{1,0:T(8,128)(2,1)} %bitcast.221, bf16[384,2304]{1,0:T(8,128)(2,1)} %bitcast.242, f32[2,2304]{1,0:T(2,128)} %reshape.456.bias_ref, ...), custom_call_target="tpu_custom_call" | custom-call | flops 18119393280 | bytes 30000000 | tf_op jit(solution)/shard_map/gru_backward/pallas_call | solution.py:195
  479.0 32.9 %collective-permute-done.14 = bf16[576,1536]{1,0:T(8,128)(2,1)} collective-permute-done((bf16[576,1536]{1,0:T(8,128)(2,1)}, bf16[576,1536]{1,0:T(8,128)(2,1)}, u32[]{:S(2)}, u32[]{:S(2)}) %collective-permute-start.14) | collective-permute-done | bytes 1769504 | tf_op jit(solution)/shard_map/ppermute | solution.py:381
  517.6 11.4 %convolution_convert_fusion.5 = bf16[2048,768]{1,0:T(8,128)(2,1)} fusion(bf16[2048,2304]{1,0:T(8,128)(2,1)} %bitcast.281, bf16[768,2304]{1,0:T(8,128)(2,1)S(1)} %bitcast.222), kind=kOutput, calls=%fused_computation.24 | convolution fusion | flops 7249330176 | bytes 16121856 | tf_op jit(solution)/shard_map/dot_general | solution.py:27
  529.1 9.8 %convolution_convert_fusion.1 = bf16[2304,768]{0,1:T(8,128)(2,1)} fusion(bf16[2048,2304]{1,0:T(8,128)(2,1)S(1)} %bitcast.284, bf16[2048,768]{1,0:T(8,128)(2,1)S(1)} %bitcast.227), kind=kOutput, calls=%fused_computation.9 | convolution fusion | flops 7249526784 | bytes 16121856 | tf_op jit(solution)/shard_map/dot_general | solution.py:23
  543.7 5.0 convolution_convert_fusion.2
  548.7 90.6 %sum_grads.1 = (bf16[96,3072]{1,0:T(8,128)(2,1)}, bf16[96,2304]{1,0:T(8,128)(2,1)}, bf16[96,2304]{1,0:T(8,128)(2,1)}, bf16[48,2304]{1,0:T(8,128)(2,1)}, bf16[96,...) custom-call(bf16[4,2,96,3072]{3,2,1,0:T(8,128)(2,1)} %bitcast.217, ...), custom_call_target="tpu_custom_call" | custom-call | tf_op jit(solution)/shard_map/sum_grads/pallas_call | solution.py:691
  674.9 6.8 collective-permute-done.18
  (415 shorter events, 243.6 us)
Async XLA Ops:
  7.2 67.1 %all-gather.8.cloned.1.call-start = ((), (), s32[]{:S(2)}) async-start(), calls=%async_computation.11 | async-start | bytes 10285056 | tf_op jit(solution)/shard_map/all_gather | solution.py:749
  14.0 163.5 %all-gather.10.cloned.1.call-start = ((), (), s32[]{:S(2)}) async-start(), calls=%async_computation.12 | async-start | bytes 14708736 | tf_op jit(solution)/shard_map/all_gather | solution.py:749
  21.7 230.7 %all-gather.6.cloned.1.call-start = ((), (), s32[]{:S(2)}) async-start(), calls=%async_computation.7 | async-start | bytes 15925248 | tf_op jit(solution)/shard_map/all_gather | solution.py:855
  23.2 66.2 %collective-permute-start = (bf16[2,256,768]{2,1,0:T(8,128)(2,1)}, bf16[2,256,768]{2,1,0:T(8,128)(2,1)}, u32[]{:S(2)}, u32[]{:S(2)}) collective-permute-start(bf16[2,256,768]{2,1,0:T(8,128)(2,1)} %param.27), channel_id=1, source_target_pairs={{0,4},{4,0},{8,12},{12,8},{16,20},{20,16},{24,28},{28,24},{1,5},{5... | collective-permute-start | bytes 2359304 | tf_op jit(solution)/shard_map/ppermute | solution.py:338
  23.7 65.7 %collective-permute-start.1 = (bf16[2,256,768]{2,1,0:T(8,128)(2,1)}, bf16[2,256,768]{2,1,0:T(8,128)(2,1)}, u32[]{:S(2)}, u32[]{:S(2)}) collective-permute-start(bf16[2,256,768]{2,1,0:T(8,128)(2,1)} %param.28), channel_id=1, source_target_pairs={{0,4},{4,0},{8,12},{12,8},{16,20},{20,16},{24,28},{28,24},{1,5},{5... | collective-permute-start | bytes 2359304 | tf_op jit(solution)/shard_map/ppermute | solution.py:338
  96.1 59.1 %all-to-all-start = ((bf16[4,2,256,576]{2,3,1,0:T(8,128)(2,1)}), bf16[4,2,256,576]{2,3,1,0:T(8,128)(2,1)S(1)}, u32[]{:S(2)}, u32[]{:S(2)}) async-start(bf16[4,2,256,576]{2,3,1,0:T(8,128)(2,1)} %copy.142), calls=%async_computation | async-start | bytes 4718592 | tf_op jit(solution)/shard_map/all_to_all | solution.py:327
  110.0 102.9 %collective-permute-start.3 = (bf16[2,256,768]{2,1,0:T(8,128)(2,1)S(1)}, bf16[2,256,768]{2,1,0:T(8,128)(2,1)}, u32[]{:S(2)}, u32[]{:S(2)}) collective-permute-start(bf16[2,256,768]{2,1,0:T(8,128)(2,1)S(1)} %get-tuple-element.103), channel_id=1, source_target_pairs={{0,16},{4,20},{8,24},{12,28},{16,0},{20,4},{24,8},{28,12},{1,17},{... | collective-permute-start | bytes 2359304 | tf_op jit(solution)/shard_map/ppermute | solution.py:338
  111.1 101.8 %collective-permute-start.2 = (bf16[2,256,768]{2,1,0:T(8,128)(2,1)}, bf16[2,256,768]{2,1,0:T(8,128)(2,1)}, u32[]{:S(2)}, u32[]{:S(2)}) collective-permute-start(bf16[2,256,768]{2,1,0:T(8,128)(2,1)} %get-tuple-element.101), channel_id=1, source_target_pairs={{0,8},{4,12},{8,0},{12,4},{16,24},{20,28},{24,16},{28,20},{1,9},{5... | collective-permute-start | bytes 2359304 | tf_op jit(solution)/shard_map/ppermute | solution.py:338
  179.8 30.8 %all-to-all-start.1 = ((bf16[4,2,256,192]{2,3,1,0:T(8,128)(2,1)}), bf16[4,2,256,192]{2,3,1,0:T(8,128)(2,1)}, u32[]{:S(2)}, u32[]{:S(2)}) async-start(bf16[4,2,256,192]{2,3,1,0:T(8,128)(2,1)} %copy.146), calls=%async_computation.1 | async-start | bytes 1572864 | tf_op jit(solution)/shard_map/all_to_all | solution.py:327
  184.0 244.2 %reduce-scatter.4.cloned.1.call-start = ((), (), s32[]{:S(2)}) async-start(), calls=%async_computation.8 | async-start | bytes 15925248 | tf_op jit(solution)/shard_map/reduce_scatter | solution.py:815
  237.9 32.6 %collective-permute-start.8 = (bf16[2,256,768]{2,1,0:T(8,128)(2,1)}, bf16[2,256,768]{2,1,0:T(8,128)(2,1)}, u32[]{:S(2)}, u32[]{:S(2)}) collective-permute-start(bf16[2,256,768]{2,1,0:T(8,128)(2,1)} %broadcast_select_fusion.7), channel_id=1, source_target_pairs={{0,16},{4,20},{8,24},{12,28},{16,0},{20,4},{24,8},{28,12},{1,17},{... | collective-permute-start | bytes 2359304 | tf_op jit(solution)/shard_map/ppermute | solution.py:338
  239.2 31.4 %collective-permute-start.9 = (bf16[2,256,768]{2,1,0:T(8,128)(2,1)}, bf16[2,256,768]{2,1,0:T(8,128)(2,1)}, u32[]{:S(2)}, u32[]{:S(2)}) collective-permute-start(bf16[2,256,768]{2,1,0:T(8,128)(2,1)} %broadcast_select_fusion.11), channel_id=1, source_target_pairs={{0,8},{4,12},{8,0},{12,4},{16,24},{20,28},{24,16},{28,20},{1,9},{5... | collective-permute-start | bytes 2359304 | tf_op jit(solution)/shard_map/ppermute | solution.py:338
  290.6 258.0 %reduce-scatter.8.cloned.1.call-start = ((), (), s32[]{:S(2)}) async-start(), calls=%async_computation.10 | async-start | bytes 2654208 | tf_op jit(solution)/shard_map/reduce_scatter | solution.py:815
  295.7 16.3 %collective-permute-start.12 = (bf16[2,1,1536]{2,1,0:T(2,128)(2,1)S(1)}, bf16[2,1,1536]{2,1,0:T(2,128)(2,1)S(1)}, u32[]{:S(2)}, u32[]{:S(2)}) collective-permute-start(bf16[2,1,1536]{2,1,0:T(2,128)(2,1)S(1)} %get-tuple-element.212), channel_id=1, source_target_pairs={{1,0},{2,1},{3,2},{5,4},{6,5},{7,6},{9,8},{10,9},{11,10},{13,12},{... | collective-permute-start | bytes 18440 | tf_op jit(solution)/shard_map/ppermute | solution.py:371
  304.6 58.7 %collective-permute-start.11 = (bf16[2,256,768]{2,1,0:T(8,128)(2,1)}, bf16[2,256,768]{2,1,0:T(8,128)(2,1)}, u32[]{:S(2)}, u32[]{:S(2)}) collective-permute-start(bf16[2,256,768]{2,1,0:T(8,128)(2,1)} %get-tuple-element.126), channel_id=1, source_target_pairs={{0,16},{4,20},{8,24},{12,28},{16,0},{20,4},{24,8},{28,12},{1,17},{... | collective-permute-start | bytes 2359304 | tf_op jit(solution)/shard_map/ppermute | solution.py:338
  305.2 58.1 %collective-permute-start.10 = (bf16[2,256,768]{2,1,0:T(8,128)(2,1)}, bf16[2,256,768]{2,1,0:T(8,128)(2,1)}, u32[]{:S(2)}, u32[]{:S(2)}) collective-permute-start(bf16[2,256,768]{2,1,0:T(8,128)(2,1)} %get-tuple-element.124), channel_id=1, source_target_pairs={{0,8},{4,12},{8,0},{12,4},{16,24},{20,28},{24,16},{28,20},{1,9},{5... | collective-permute-start | bytes 2359304 | tf_op jit(solution)/shard_map/ppermute | solution.py:338
  326.2 222.5 %reduce-scatter.6.cloned.1.call-start = ((), (), s32[]{:S(2)}) async-start(), calls=%async_computation.9 | async-start | bytes 5308416 | tf_op jit(solution)/shard_map/reduce_scatter | solution.py:815
  365.6 23.8 %all-to-all-start.2 = ((bf16[4,2,256,192]{2,3,1,0:T(8,128)(2,1)}), bf16[4,2,256,192]{2,3,1,0:T(8,128)(2,1)S(1)}, u32[]{:S(2)}, u32[]{:S(2)}) async-start(bf16[4,2,256,192]{2,3,1,0:T(8,128)(2,1)} %copy.153), calls=%async_computation.3 | async-start | bytes 1572864 | tf_op jit(solution)/shard_map/all_to_all | solution.py:327
  432.5 106.3 %all-to-all-start.3 = ((bf16[4,2,256,576]{2,3,1,0:T(8,128)(2,1)}), bf16[4,2,256,576]{2,3,1,0:T(8,128)(2,1)S(1)}, u32[]{:S(2)}, u32[]{:S(2)}) async-start(bf16[4,2,256,576]{2,3,1,0:T(8,128)(2,1)} %copy.156), calls=%async_computation.4 | async-start | bytes 4718592 | tf_op jit(solution)/shard_map/all_to_all | solution.py:327
  436.2 75.7 %collective-permute-start.14 = (bf16[576,1536]{1,0:T(8,128)(2,1)}, bf16[576,1536]{1,0:T(8,128)(2,1)}, u32[]{:S(2)}, u32[]{:S(2)}) collective-permute-start(bf16[576,1536]{1,0:T(8,128)(2,1)} %reduce-scatter.4.cloned.1.call-done), channel_id=1, source_target_pairs={{0,1},{3,2},{4,5},{7,6},{8,9},{11,10},{12,13},{15,14},{16,17},{19,... | collective-permute-start | bytes 5308424 | tf_op jit(solution)/shard_map/ppermute | solution.py:381
  515.8 123.5 %collective-permute-start.17 = (bf16[576,1536]{1,0:T(8,128)(2,1)}, bf16[576,1536]{1,0:T(8,128)(2,1)}, u32[]{:S(2)}, u32[]{:S(2)}) collective-permute-start(bf16[576,1536]{1,0:T(8,128)(2,1)} %add.273), channel_id=1, source_target_pairs={{1,2},{2,1},{5,6},{6,5},{9,10},{10,9},{13,14},{14,13},{17,18},{18,... | collective-permute-start | bytes 5308424 | tf_op jit(solution)/shard_map/ppermute | solution.py:381
  641.8 39.9 %collective-permute-start.18 = (bf16[576,1536]{1,0:T(8,128)(2,1)S(1)}, bf16[576,1536]{1,0:T(8,128)(2,1)}, u32[]{:S(2)}, u32[]{:S(2)}) collective-permute-start(bf16[576,1536]{1,0:T(8,128)(2,1)S(1)} %add.275), channel_id=1, source_target_pairs={{1,0},{2,3},{5,4},{6,7},{9,8},{10,11},{13,12},{14,15},{17,16},{18,... | collective-permute-start | bytes 5308424 | tf_op jit(solution)/shard_map/ppermute | solution.py:381
  647.8 22.3 %collective-permute-start.15 = (bf16[2,256,768]{2,1,0:T(8,128)(2,1)}, bf16[2,256,768]{2,1,0:T(8,128)(2,1)}, u32[]{:S(2)}, u32[]{:S(2)}) collective-permute-start(bf16[2,256,768]{2,1,0:T(8,128)(2,1)} %broadcast_select_fusion.5), channel_id=1, source_target_pairs={{0,16},{4,20},{8,24},{12,28},{16,0},{20,4},{24,8},{28,12},{1,17},{... | collective-permute-start | bytes 2359304 | tf_op jit(solution)/shard_map/ppermute | solution.py:338
  648.8 21.3 %collective-permute-start.16 = (bf16[2,256,768]{2,1,0:T(8,128)(2,1)}, bf16[2,256,768]{2,1,0:T(8,128)(2,1)}, u32[]{:S(2)}, u32[]{:S(2)}) collective-permute-start(bf16[2,256,768]{2,1,0:T(8,128)(2,1)} %broadcast_select_fusion.9), channel_id=1, source_target_pairs={{0,8},{4,12},{8,0},{12,4},{16,24},{20,28},{24,16},{28,20},{1,9},{5... | collective-permute-start | bytes 2359304 | tf_op jit(solution)/shard_map/ppermute | solution.py:338
  (72 other events, 437.1 us)
Sparse Core Ops, SparseCore 0:
  14.1 60.1 all-gather.7
  76.2 90.4 all-gather.9
  168.6 83.7 all-gather.5
  290.7 100.8 reduce-scatter.3
  394.8 42.3 reduce-scatter.7
  440.5 53.7 reduce-scatter.5
where the time goes:
time: 700 us; the launch traced here: 692 us
  Pallas kernels  205 us (29%)
  waiting for transfers between devices  130 us (19%)
  matrix products  122 us (17%)
  local copies, waits for them, and re-layouts  99.8 us (14%)
  other arithmetic  74.6 us (11%)
  starting transfers between devices  46.2 us (7%)
  between operations  15.5 us (2%)
    pallas_call x1, Pallas kernels, sum_grads(): pl.pallas_call(partial(sum_kernel, spans, pre_spans, late, pre, high, lag...  90.6 us
    dot_general x10, matrix products, dot_right(): lax.dot_general(left, right, (((1,), (1,)), ((), ())), preferred_element_...  50.5 us
    all_gather x2, waiting for transfers between devices, pack(): return lax.all_gather(jnp.concatenate(pieces, axis=0), 'dp', axis=0)  46.2 us
    ppermute x3, waiting for transfers between devices, line_sum(): other = lax.ppermute(value, 'seq', LINE[step])  39.7 us
    dot_general x8, matrix products, dot_left(): lax.dot_general(left, right, (((0,), (0,)), ((), ())), preferred_element_...  38.5 us
    pallas_call x1, Pallas kernels, attention_backward(): pl.pallas_call(partial(attention_backward_kernel, per), grid_spec=pltpu.P...  37.5 us
    pallas_call x1, Pallas kernels, gru_backward(): pl.pallas_call(gru_backward_kernel, grid=(rows // high,), in_specs=gru_sp...  36.7 us
    dot_general x7, matrix products, dot_plain(): return jnp.dot(left, right, preferred_element_type=F32)  32.9 us
  transfers between devices with their start and end apart: 29, of which 9 were waited for; matrix products, arithmetic and copies ran while one was open for 37% of the time, Pallas kernels for 30%

commit v1 on v0

--- a/solution.py
+++ b/solution.py
@@ -372,16 +372,14 @@
     return low, high
 
 
-LINE = ([(0, 1), (3, 2)], [(1, 2), (2, 1)], [(1, 0), (2, 3)])
+LINE = ([(0, 1), (3, 2)], [(1, 2), (2, 1)])
 
 
 def line_sum(value, step):
     if lax.axis_size("seq") != 4:
         return lax.psum(value, "seq") if step == 0 else value
     other = lax.ppermute(value, "seq", LINE[step])
-    if step < 2:
-        return value + other
-    return jnp.where((lax.axis_index("seq") % 3) == 0, other, value)
+    return value + other
 
 
 def shifted(block, low, high):
@@ -405,12 +403,15 @@
     whole = len(spans)
     count = whole + len(pre_spans)
     total = late + pre
-    ins, outs = refs[:count], refs[count : 2 * count]
+    ins, middle_ref = refs[:count], refs[count]
+    outs, ends_ref = refs[count + 1 : 2 * count + 1], refs[2 * count + 1]
+    refs = refs[2:]
     own, rc, sc, s1a, s1b, r1a, r1b, r2a, r2b, s2, rz, sz, rm, tot, ready = refs[
         2 * count : 2 * count + 15
     ]
     sems = refs[2 * count + 15]
     credits = refs[2 * count + 16]
+    ends_sems = refs[2 * count + 17]
     half = WIDE // 2
     dp, z = lax.axis_index("dp"), lax.axis_index("seq")
     core, x, y = dp % 2, (dp // 2) % 2, dp // 4
@@ -529,6 +530,19 @@
         @pl.when((k >= 0) & (k < total))
         def _():
             run(k, lax.rem(jnp.maximum(k, 0), slots))
+
+    ends = pltpu.make_async_remote_copy(
+        src_ref=middle_ref,
+        dst_ref=ends_ref,
+        send_sem=ends_sems.at[0],
+        recv_sem=ends_sems.at[1],
+        device_id=at_outer,
+        device_id_type=pl.DeviceIdType.MESH,
+    )
+
+    @pl.when(inner)
+    def _():
+        ends.start()
 
     first = ins[0].at[:, core, pl.ds(0, high), pl.ds(0, WIDE)]
     final = outs[0].at[pl.ds(0, high), pl.ds(0, WIDE)]
@@ -678,8 +692,16 @@
         stage(t - 5 * lag, go_final)
         stage(t - 6 * lag, finish)
 
-
-def sum_grads(grads, pres, high=48, lag=3, slots=6):
+    @pl.when(inner)
+    def _():
+        ends.wait_send()
+
+    @pl.when(outer)
+    def _():
+        ends.wait_recv()
+
+
+def sum_grads(grads, pres, middle, high=48, lag=3, slots=6):
     shapes = [(grad.shape[0] // 8, grad.shape[1]) for grad in grads]
     pre_shapes = [grad.shape for grad in pres]
     spans, late = sum_plan(shapes, high)
@@ -690,9 +712,9 @@
     shapes = shapes + pre_shapes
     return pl.pallas_call(
         partial(sum_kernel, spans, pre_spans, late, pre, high, lag, slots),
-        in_specs=[anywhere] * len(shapes),
-        out_specs=[anywhere] * len(shapes),
-        out_shape=[jax.ShapeDtypeStruct(shape, BF) for shape in shapes],
+        in_specs=[anywhere] * (len(shapes) + 1),
+        out_specs=[anywhere] * (len(shapes) + 1),
+        out_shape=[jax.ShapeDtypeStruct(shape, BF) for shape in shapes + [middle.shape]],
         scratch_shapes=[
             pltpu.VMEM((slots, 4, high, WIDE), BF),
             pltpu.VMEM((slots, 4, high, WIDE), BF),
@@ -711,10 +733,11 @@
             pltpu.VMEM((slots, high, WIDE), BF),
             pltpu.SemaphoreType.DMA((20, slots)),
             pltpu.SemaphoreType.REGULAR((8,)),
+            pltpu.SemaphoreType.DMA((2,)),
         ],
         compiler_params=pltpu.CompilerParams(collective_id=1, has_side_effects=True),
         name="sum_grads",
-    )(*blocks, *pres)
+    )(*blocks, *pres, middle)
 
 
 def heads_first(weight, parts):
@@ -790,11 +813,15 @@
     return [lax.psum(part, "seq") for part in outs + list(pres)]
 
 
-def reduce_grads(big, pres, small):
+def reduce_grads(big, pres, middle, small):
     groups = lax.axis_size("dp")
     ours = groups == 8 and lax.axis_size("seq") == 4
     grads = [grad.astype(BF) for grad in big] + [pack_small(small, groups, 48)]
-    outs = sum_grads(grads, pres) if ours else sum_grads_plain(grads, pres)
+    if ours:
+        *outs, ends = sum_grads(grads, pres, middle)
+        middle = jnp.where((lax.axis_index("seq") % 3) == 0, ends, middle)
+    else:
+        outs = sum_grads_plain(grads, pres)
     tail = outs[len(big)]
     sizes = []
     for piece in small:
@@ -808,7 +835,8 @@
         vectors.append(part.reshape(many, size).T if matrix else part)
         at += many * size
     bigs = [piece.astype(F32) for piece in outs[: len(big)]]
-    return bigs, [piece.astype(F32) for piece in outs[len(big) + 1 :]], vectors
+    early = [piece.astype(F32) for piece in outs[len(big) + 1 :]]
+    return bigs, early + [middle.astype(F32)], vectors
 
 
 def scatter_sum(grad):
@@ -946,21 +974,23 @@
     grad_out = dot_left(context, d_attend)
     d_context = dot_right(d_attend, w_out).astype(BF)
     d_context = d_context.reshape(seqs, local, parts, per * HEAD).transpose(2, 0, 1, 3)
-    d_project = attention_backward(qkv, exchange(d_context), own_lengths, per)
+    d_context, sum_conv, grad_in, grad_out = lax.optimization_barrier(
+        (exchange(d_context), sum_conv, grad_in.astype(BF), grad_out.astype(BF))
+    )
+    sum_conv = line_sum(sum_conv, 0)
+    d_project = attention_backward(qkv, d_context, own_lengths, per)
     sum_conv, d_char_state, d_project = lax.optimization_barrier((sum_conv, d_char_state, d_project))
+    sum_conv = line_sum(sum_conv, 1)
     d_project = exchange(d_project)
-    sum_conv = line_sum(sum_conv, 0)
-    d_project = d_project.transpose(1, 2, 0, 3).reshape(rows, 3 * width)
 
     d_gates, grad_gru_h, grad_gru_bias = gru_backward(
         counts, row_chars, gru_x, gru_h, gru_bias, d_char_state
     )
-    sum_conv, d_gates = lax.optimization_barrier((sum_conv, d_gates))
-    sum_conv = line_sum(sum_conv, 1)
     d_gates = d_gates.reshape(NCHAR * rows, 2 * three)
     grad_gru_x = dot_left(flat_chars, d_gates)
     chars_back = dot_right(d_gates, gru_x).astype(BF)
-    chars_back, sum_conv = lax.optimization_barrier((chars_back, sum_conv))
+    chars_back, d_project, sum_conv = lax.optimization_barrier((chars_back, d_project, sum_conv))
+    d_project = d_project.transpose(1, 2, 0, 3).reshape(rows, 3 * width)
     chars_back = chars_back.reshape(NCHAR, seqs, local, width).transpose(1, 2, 0, 3)
 
     grad_qkv = dot_left(flat_tokens, d_project)
@@ -982,12 +1012,11 @@
             column_sum(d_char_side),
         ],
     )
-    big, early, small = reduce_grads(big, (sum_back, sum_blend), small)
+    big, early, small = reduce_grads(big, (sum_back, sum_blend), sum_conv, small)
     outs, big[-1] = lax.optimization_barrier((outs, big[-1]))
     outs = relocate_last(masks, outs, 2, big[-1])
     g_in, g_qkv, g_gru_x, g_gru_h, g_out = big
-    g_back, g_blend = early
-    g_conv = line_sum(sum_conv, 2).astype(F32)
+    g_back, g_blend, g_conv = early
     g_b_qv, g_b_in, g_gru_bias, g_conv_b, g_gain, g_shift, g_rows = small
     return (
         outs[0],

time: 700 us -> 702 us (level)
  waiting for transfers between devices: 130 us -> 117 us
  local copies, waits for them, and re-layouts: 99.8 us -> 111 us
  Pallas kernels: 205 us -> 215 us
  other arithmetic: 74.6 us -> 67.3 us
    ppermute x3 -> x2, waiting for transfers between devices: 39.7 us -> 0.01 us  [line_sum(): other = lax.ppermute(value, 'seq', LINE[step])]
    all_to_all x4, waiting for transfers between devices: 32 us -> 52.2 us  [exchange(): return lax.all_to_all(blocks, 'seq', split_axis=0, concat_axis=0)]
    pallas_call x1, Pallas kernels: 90.6 us -> 101 us  [sum_grads(): pl.pallas_call(partial(sum_kernel, spans, pre_spans, late, pre, high, lag...]
    unnamed x154 -> x174, local copies, waits for them, and re-layouts: 28 us -> 33.4 us
  transfers between devices with their start and end apart: 29 -> 28, of which waited for: 9 -> 10; matrix products, arithmetic and copies ran while one was open for 37% -> 35% of each run, Pallas kernels for 30% -> 17%
where the time goes in v1:
time: 702 us; the launch traced here: 694 us
  Pallas kernels  215 us (31%)
  matrix products  123 us (18%)
  waiting for transfers between devices  117 us (17%)
  local copies, waits for them, and re-layouts  111 us (16%)
  other arithmetic  67.3 us (10%)
  starting transfers between devices  44.4 us (6%)
  between operations  15.6 us (2%)
    pallas_call x1, Pallas kernels, sum_grads(): pl.pallas_call(partial(sum_kernel, spans, pre_spans, late, pre, high, lag...  101 us
    all_to_all x4, waiting for transfers between devices, exchange(): return lax.all_to_all(blocks, 'seq', split_axis=0, concat_axis=0)  52.2 us
    dot_general x10, matrix products, dot_right(): lax.dot_general(left, right, (((1,), (1,)), ((), ())), preferred_element_...  50.8 us
    all_gather x2, waiting for transfers between devices, pack(): return lax.all_gather(jnp.concatenate(pieces, axis=0), 'dp', axis=0)  46.2 us
    dot_general x8, matrix products, dot_left(): lax.dot_general(left, right, (((0,), (0,)), ((), ())), preferred_element_...  39.3 us
    pallas_call x1, Pallas kernels, attention_backward(): pl.pallas_call(partial(attention_backward_kernel, per), grid_spec=pltpu.P...  37.4 us
    pallas_call x1, Pallas kernels, gru_backward(): pl.pallas_call(gru_backward_kernel, grid=(rows // high,), in_specs=gru_sp...  37.4 us
    unnamed x174, local copies, waits for them, and re-layouts  33.4 us
  transfers between devices with their start and end apart: 28, of which 10 were waited for; matrix products, arithmetic and copies ran while one was open for 35% of the time, Pallas kernels for 17%

profile of v1, /device:TPU:0, one launch (start us, length us, event | category | flops | bytes accessed | tf_op | source)
XLA Modules:
  0.0 694.0 jit_solution(12343531936310437153)
XLA Ops:
  28.2 46.2 %all-gather.8.cloned.1.call-done = bf16[1984,2304]{1,0:T(8,128)(2,1)} async-done(((bf16[248,2304]{1,0:T(8,128)(2,1)}), bf16[1984,2304]{1,0:T(8,128)(2,1)}) %all-gather.8.cloned.1.call-update) | async-done | bytes 9142288 | tf_op jit(solution)/shard_map/all_gather | solution.py:772
  75.4 5.4 fusion.68
  89.4 5.0 reshape.453
  112.1 20.0 %gru_forward.1 = f32[512,768]{1,0:T(8,128)} custom-call(s32[512,1]{1,0:T(8,128)} %bitcast.257, bf16[4,512,768]{2,1,0:T(8,128)(2,1)} %bitcast.225, bf16[768,2304]{1,0:T(8,128)(2,1)} %bitcast.220, bf16[384,2304]{1,0:T(8,128)(2,1)} %bitcast.242, f32[2,2304]{1,0:T(2,128)} %reshape.456.bias_ref), custom_call_target="tpu_custom_call" | custom-call | flops 10871635968 | bytes 10000000 | tf_op jit(solution)/shard_map/gru_forward/pallas_call | solution.py:104
  132.1 23.1 %all-to-all-done = bf16[4,2,256,576]{2,3,1,0:T(8,128)(2,1)S(1)} async-done(((bf16[4,2,256,576]{2,3,1,0:T(8,128)(2,1)}), bf16[4,2,256,576]{2,3,1,0:T(8,128)(2,1)S(1)}, u32[]{:S(2)}, u32[]{:S(2)}) %all-to-all-start) | async-done | bytes 2359328 | tf_op jit(solution)/shard_map/all_to_all | solution.py:327
  157.8 19.7 %attend_forward.1 = bf16[4,2,256,192]{3,2,1,0:T(8,128)(2,1)} custom-call(s32[2]{0:T(128)} %dynamic_slice.3.len_ref, bf16[4,2,256,576]{3,2,1,0:T(8,128)(2,1)} %copy.145.qkv_ref), custom_call_target="tpu_custom_call" | custom-call | tf_op jit(solution)/shard_map/attend_forward/pallas_call | solution.py:249
  191.0 6.7 fusion.67
  215.8 7.3 %fusion.3 = (f32[512,3072]{1,0:T(8,128)}, bf16[512,3072]{1,0:T(8,128)(2,1)S(1)}) fusion(f32[3072]{0:T(1024)S(1)} %add.232, bf16[768,3072]{1,0:T(8,128)(2,1)S(1)} %bitcast.211, f32[512,768]{1,0:T(8,128)S(1)} %get-tuple-element.244, f32[768]{0:T(1024)S(1)} %add.229, f32[768]{0:T(1024)S(1)} %mul.297, f32[512]{0:T(512)S(1)} %add_rsqrt_fusion.3, ...), kind=kOutput, calls=%fused_computation.5 | convolution fusion | flops 2435186688 | bytes 15751168 | tf_op jit(solution)/shard_map/dot_general | solution.py:19
  243.6 8.7 %all-gather.6.cloned.1.call-done = bf16[4608,1536]{1,0:T(8,128)(2,1)} async-done(((bf16[576,1536]{1,0:T(8,128)(2,1)}), bf16[4608,1536]{1,0:T(8,128)(2,1)}) %all-gather.6.cloned.1.call-update) | async-done | bytes 14155792 | tf_op jit(solution)/shard_map/all_gather | solution.py:883
  252.3 14.4 %fusion.21 = (f32[512,1536]{1,0:T(8,128)S(1)}, f32[512,1536]{1,0:T(8,128)S(1)}) fusion(f32[1536]{0:T(1024)S(1)} %add.252, bf16[4608,1536]{1,0:T(8,128)(2,1)} %all-gather.6.cloned.1.call-done, bf16[512,1536]{1,0:T(8,128)(2,1)} %bitcast.246, bf16[512,1536]{1,0:T(8,128)(2,1)S(1)} %bitcast.191, bf16[512,1536]{1,0:T(8,128)(2,1)} %bitcast.244), kind=kOutput, calls=%fused_computation.31 | convolution fusion | flops 7269777408 | bytes 25171968 | tf_op jit(solution)/shard_map/dot_general | solution.py:19
  279.6 10.9 %convolution_convert_fusion = bf16[4608,1536]{1,0:T(8,128)(2,1)} fusion(bf16[512,1536]{1,0:T(8,128)(2,1)S(1)} %fusion.22, bf16[512,1536]{1,0:T(8,128)(2,1)S(1)} %bitcast.247, bf16[512,1536]{1,0:T(8,128)(2,1)S(1)} %bitcast.192, bf16[512,1536]{1,0:T(8,128)(2,1)S(1)} %bitcast.245), kind=kOutput, calls=%fused_computation | convolution fusion | flops 7268990976 | bytes 20447232 | tf_op jit(solution)/shard_map/dot_general | solution.py:23
  304.1 5.3 fusion.6
  335.8 7.6 %fusion.80 = (bf16[3072]{0:T(1024)(128)(2,1)S(1)}, bf16[512,3072]{1,0:T(8,128)(2,1)S(1)}) fusion(f32[512,3072]{1,0:T(8,128)} %get-tuple-element.126, bf16[512,768]{1,0:T(8,128)(2,1)} %copy-done.22, bf16[3072,768]{1,0:T(8,128)(2,1)} %bitcast.213), kind=kOutput, calls=%fused_computation.206 | convolution fusion | flops 2420634624 | bytes 14948352 | tf_op jit(solution)/shard_map/dot_general | solution.py:27
  343.5 6.7 multiply_reduce_fusion.1
  366.1 6.6 convolution_convert_fusion.3
  374.5 11.4 %all-to-all-done.2 = bf16[4,2,256,192]{2,3,1,0:T(8,128)(2,1)} async-done(((bf16[4,2,256,192]{2,3,1,0:T(8,128)(2,1)}), bf16[4,2,256,192]{2,3,1,0:T(8,128)(2,1)}, u32[]{:S(2)}, u32[]{:S(2)}) %all-to-all-start.2) | async-done | bytes 786464 | tf_op jit(solution)/shard_map/all_to_all | solution.py:327
  385.9 5.6 reduce-scatter.4.cloned.1.call-done
  411.4 37.4 %attend_backward.1 = bf16[4,2,256,576]{3,2,1,0:T(8,128)(2,1)} custom-call(s32[2]{0:T(128)} %dynamic_slice.3.len_ref, bf16[4,2,256,576]{3,2,1,0:T(8,128)(2,1)} %copy.145.qkv_ref, bf16[4,2,256,192]{3,2,1,0:T(8,128)(2,1)} %copy.155.grad_ref), custom_call_target="tpu_custom_call" | custom-call | tf_op jit(solution)/shard_map/attend_backward/pallas_call | solution.py:306
  461.3 37.4 %gru_backward.1 = (bf16[4,512,2304]{2,1,0:T(8,128)(2,1)}, bf16[384,2304]{1,0:T(8,128)(2,1)}, f32[2,2304]{1,0:T(2,128)}) custom-call(s32[512,1]{1,0:T(8,128)} %bitcast.258, bf16[4,512,768]{2,1,0:T(8,128)(2,1)} %bitcast.226, bf16[768,2304]{1,0:T(8,128)(2,1)} %bitcast.221, bf16[384,2304]{1,0:T(8,128)(2,1)} %bitcast.243, f32[2,2304]{1,0:T(2,128)} %reshape.456.bias_ref, ...), custom_call_target="tpu_custom_call" | custom-call | flops 18119393280 | bytes 30000000 | tf_op jit(solution)/shard_map/gru_backward/pallas_call | solution.py:195
  499.6 12.4 %convolution_convert_fusion.5 = bf16[2048,768]{1,0:T(8,128)(2,1)} fusion(bf16[2048,2304]{1,0:T(8,128)(2,1)} %bitcast.281, bf16[768,2304]{1,0:T(8,128)(2,1)} %bitcast.222), kind=kOutput, calls=%fused_computation.24 | convolution fusion | flops 7249330176 | bytes 16121856 | tf_op jit(solution)/shard_map/dot_general | solution.py:27
  512.1 9.8 %convolution_convert_fusion.1 = bf16[2304,768]{0,1:T(8,128)(2,1)} fusion(bf16[2048,2304]{1,0:T(8,128)(2,1)S(1)} %bitcast.282, bf16[2048,768]{1,0:T(8,128)(2,1)S(1)} %bitcast.227), kind=kOutput, calls=%fused_computation.9 | convolution fusion | flops 7249526784 | bytes 16121856 | tf_op jit(solution)/shard_map/dot_general | solution.py:23
  525.5 17.8 %all-to-all-done.3 = bf16[4,2,256,576]{2,3,1,0:T(8,128)(2,1)S(1)} async-done(((bf16[4,2,256,576]{2,3,1,0:T(8,128)(2,1)}), bf16[4,2,256,576]{2,3,1,0:T(8,128)(2,1)S(1)}, u32[]{:S(2)}, u32[]{:S(2)}) %all-to-all-start.3) | async-done | bytes 2359328 | tf_op jit(solution)/shard_map/all_to_all | solution.py:327
  553.2 100.9 %sum_grads.1 = (bf16[96,3072]{1,0:T(8,128)(2,1)}, bf16[96,2304]{1,0:T(8,128)(2,1)}, bf16[96,2304]{1,0:T(8,128)(2,1)}, bf16[48,2304]{1,0:T(8,128)(2,1)}, bf16[96,...) custom-call(bf16[4,2,96,3072]{3,2,1,0:T(8,128)(2,1)} %bitcast.217, ...), custom_call_target="tpu_custom_call" | custom-call | tf_op jit(solution)/shard_map/sum_grads/pallas_call | solution.py:713
  656.1 5.2 add_convert_fusion
  (432 shorter events, 247.0 us)
Async XLA Ops:
  7.2 67.1 %all-gather.8.cloned.1.call-start = ((), (), s32[]{:S(2)}) async-start(), calls=%async_computation.11 | async-start | bytes 10285056 | tf_op jit(solution)/shard_map/all_gather | solution.py:772
  14.0 163.5 %all-gather.10.cloned.1.call-start = ((), (), s32[]{:S(2)}) async-start(), calls=%async_computation.12 | async-start | bytes 14708736 | tf_op jit(solution)/shard_map/all_gather | solution.py:772
  21.7 230.6 %all-gather.6.cloned.1.call-start = ((), (), s32[]{:S(2)}) async-start(), calls=%async_computation.7 | async-start | bytes 15925248 | tf_op jit(solution)/shard_map/all_gather | solution.py:883
  23.2 66.2 %collective-permute-start = (bf16[2,256,768]{2,1,0:T(8,128)(2,1)}, bf16[2,256,768]{2,1,0:T(8,128)(2,1)}, u32[]{:S(2)}, u32[]{:S(2)}) collective-permute-start(bf16[2,256,768]{2,1,0:T(8,128)(2,1)} %param.27), channel_id=1, source_target_pairs={{0,4},{4,0},{8,12},{12,8},{16,20},{20,16},{24,28},{28,24},{1,5},{5... | collective-permute-start | bytes 2359304 | tf_op jit(solution)/shard_map/ppermute | solution.py:338
  23.8 65.6 %collective-permute-start.1 = (bf16[2,256,768]{2,1,0:T(8,128)(2,1)}, bf16[2,256,768]{2,1,0:T(8,128)(2,1)}, u32[]{:S(2)}, u32[]{:S(2)}) collective-permute-start(bf16[2,256,768]{2,1,0:T(8,128)(2,1)} %param.28), channel_id=1, source_target_pairs={{0,4},{4,0},{8,12},{12,8},{16,20},{20,16},{24,28},{28,24},{1,5},{5... | collective-permute-start | bytes 2359304 | tf_op jit(solution)/shard_map/ppermute | solution.py:338
  96.1 59.1 %all-to-all-start = ((bf16[4,2,256,576]{2,3,1,0:T(8,128)(2,1)}), bf16[4,2,256,576]{2,3,1,0:T(8,128)(2,1)S(1)}, u32[]{:S(2)}, u32[]{:S(2)}) async-start(bf16[4,2,256,576]{2,3,1,0:T(8,128)(2,1)} %copy.142), calls=%async_computation | async-start | bytes 4718592 | tf_op jit(solution)/shard_map/all_to_all | solution.py:327
  110.0 102.9 %collective-permute-start.3 = (bf16[2,256,768]{2,1,0:T(8,128)(2,1)S(1)}, bf16[2,256,768]{2,1,0:T(8,128)(2,1)}, u32[]{:S(2)}, u32[]{:S(2)}) collective-permute-start(bf16[2,256,768]{2,1,0:T(8,128)(2,1)S(1)} %get-tuple-element.107), channel_id=1, source_target_pairs={{0,16},{4,20},{8,24},{12,28},{16,0},{20,4},{24,8},{28,12},{1,17},{... | collective-permute-start | bytes 2359304 | tf_op jit(solution)/shard_map/ppermute | solution.py:338
  111.1 101.8 %collective-permute-start.2 = (bf16[2,256,768]{2,1,0:T(8,128)(2,1)}, bf16[2,256,768]{2,1,0:T(8,128)(2,1)}, u32[]{:S(2)}, u32[]{:S(2)}) collective-permute-start(bf16[2,256,768]{2,1,0:T(8,128)(2,1)} %get-tuple-element.105), channel_id=1, source_target_pairs={{0,8},{4,12},{8,0},{12,4},{16,24},{20,28},{24,16},{28,20},{1,9},{5... | collective-permute-start | bytes 2359304 | tf_op jit(solution)/shard_map/ppermute | solution.py:338
  179.8 30.9 %all-to-all-start.1 = ((bf16[4,2,256,192]{2,3,1,0:T(8,128)(2,1)}), bf16[4,2,256,192]{2,3,1,0:T(8,128)(2,1)}, u32[]{:S(2)}, u32[]{:S(2)}) async-start(bf16[4,2,256,192]{2,3,1,0:T(8,128)(2,1)} %copy.146), calls=%async_computation.1 | async-start | bytes 1572864 | tf_op jit(solution)/shard_map/all_to_all | solution.py:327
  184.0 207.5 %reduce-scatter.4.cloned.1.call-start = ((), (), s32[]{:S(2)}) async-start(), calls=%async_computation.8 | async-start | bytes 15925248 | tf_op jit(solution)/shard_map/reduce_scatter | solution.py:843
  238.1 32.4 %collective-permute-start.8 = (bf16[2,256,768]{2,1,0:T(8,128)(2,1)}, bf16[2,256,768]{2,1,0:T(8,128)(2,1)}, u32[]{:S(2)}, u32[]{:S(2)}) collective-permute-start(bf16[2,256,768]{2,1,0:T(8,128)(2,1)} %broadcast_select_fusion.7), channel_id=1, source_target_pairs={{0,16},{4,20},{8,24},{12,28},{16,0},{20,4},{24,8},{28,12},{1,17},{... | collective-permute-start | bytes 2359304 | tf_op jit(solution)/shard_map/ppermute | solution.py:338
  239.3 31.2 %collective-permute-start.9 = (bf16[2,256,768]{2,1,0:T(8,128)(2,1)}, bf16[2,256,768]{2,1,0:T(8,128)(2,1)}, u32[]{:S(2)}, u32[]{:S(2)}) collective-permute-start(bf16[2,256,768]{2,1,0:T(8,128)(2,1)} %broadcast_select_fusion.11), channel_id=1, source_target_pairs={{0,8},{4,12},{8,0},{12,4},{16,24},{20,28},{24,16},{28,20},{1,9},{5... | collective-permute-start | bytes 2359304 | tf_op jit(solution)/shard_map/ppermute | solution.py:338
  290.5 262.7 %reduce-scatter.8.cloned.1.call-start = ((), (), s32[]{:S(2)}) async-start(), calls=%async_computation.10 | async-start | bytes 2654208 | tf_op jit(solution)/shard_map/reduce_scatter | solution.py:843
  295.0 14.8 %collective-permute-start.12 = (bf16[2,1,1536]{2,1,0:T(2,128)(2,1)S(1)}, bf16[2,1,1536]{2,1,0:T(2,128)(2,1)S(1)}, u32[]{:S(2)}, u32[]{:S(2)}) collective-permute-start(bf16[2,1,1536]{2,1,0:T(2,128)(2,1)S(1)} %get-tuple-element.220), channel_id=1, source_target_pairs={{1,0},{2,1},{3,2},{5,4},{6,5},{7,6},{9,8},{10,9},{11,10},{13,12},{... | collective-permute-start | bytes 18440 | tf_op jit(solution)/shard_map/ppermute | solution.py:371
  296.3 13.7 %collective-permute-start.13 = (bf16[2,1,1536]{2,1,0:T(2,128)(2,1)S(1)}, bf16[2,1,1536]{2,1,0:T(2,128)(2,1)S(1)}, u32[]{:S(2)}, u32[]{:S(2)}) collective-permute-start(bf16[2,1,1536]{2,1,0:T(2,128)(2,1)S(1)} %get-tuple-element.221), channel_id=1, source_target_pairs={{0,1},{1,2},{2,3},{4,5},{5,6},{6,7},{8,9},{9,10},{10,11},{12,13},{... | collective-permute-start | bytes 18440 | tf_op jit(solution)/shard_map/ppermute | solution.py:370
  302.3 49.7 %collective-permute-start.11 = (bf16[2,256,768]{2,1,0:T(8,128)(2,1)}, bf16[2,256,768]{2,1,0:T(8,128)(2,1)}, u32[]{:S(2)}, u32[]{:S(2)}) collective-permute-start(bf16[2,256,768]{2,1,0:T(8,128)(2,1)} %get-tuple-element.130), channel_id=1, source_target_pairs={{0,16},{4,20},{8,24},{12,28},{16,0},{20,4},{24,8},{28,12},{1,17},{... | collective-permute-start | bytes 2359304 | tf_op jit(solution)/shard_map/ppermute | solution.py:338
  302.8 49.2 %collective-permute-start.10 = (bf16[2,256,768]{2,1,0:T(8,128)(2,1)}, bf16[2,256,768]{2,1,0:T(8,128)(2,1)}, u32[]{:S(2)}, u32[]{:S(2)}) collective-permute-start(bf16[2,256,768]{2,1,0:T(8,128)(2,1)} %get-tuple-element.128), channel_id=1, source_target_pairs={{0,8},{4,12},{8,0},{12,4},{16,24},{20,28},{24,16},{28,20},{1,9},{5... | collective-permute-start | bytes 2359304 | tf_op jit(solution)/shard_map/ppermute | solution.py:338
  361.8 24.0 %all-to-all-start.2 = ((bf16[4,2,256,192]{2,3,1,0:T(8,128)(2,1)}), bf16[4,2,256,192]{2,3,1,0:T(8,128)(2,1)}, u32[]{:S(2)}, u32[]{:S(2)}) async-start(bf16[4,2,256,192]{2,3,1,0:T(8,128)(2,1)} %copy.153), calls=%async_computation.2 | async-start | bytes 1572864 | tf_op jit(solution)/shard_map/all_to_all | solution.py:327
  366.0 187.1 %reduce-scatter.6.cloned.1.call-start = ((), (), s32[]{:S(2)}) async-start(), calls=%async_computation.9 | async-start | bytes 5308416 | tf_op jit(solution)/shard_map/reduce_scatter | solution.py:843
  391.5 57.4 %collective-permute-start.14 = (bf16[576,1536]{1,0:T(8,128)(2,1)}, bf16[576,1536]{1,0:T(8,128)(2,1)}, u32[]{:S(2)}, u32[]{:S(2)}) collective-permute-start(bf16[576,1536]{1,0:T(8,128)(2,1)} %reduce-scatter.4.cloned.1.call-done), channel_id=1, source_target_pairs={{0,1},{3,2},{4,5},{7,6},{8,9},{11,10},{12,13},{15,14},{16,17},{19,... | collective-permute-start | bytes 5308424 | tf_op jit(solution)/shard_map/ppermute | solution.py:381
  453.1 68.8 %collective-permute-start.15 = (bf16[576,1536]{1,0:T(8,128)(2,1)}, bf16[576,1536]{1,0:T(8,128)(2,1)}, u32[]{:S(2)}, u32[]{:S(2)}) collective-permute-start(bf16[576,1536]{1,0:T(8,128)(2,1)} %add.272), channel_id=1, source_target_pairs={{1,2},{2,1},{5,6},{6,5},{9,10},{10,9},{13,14},{14,13},{17,18},{18,... | collective-permute-start | bytes 5308424 | tf_op jit(solution)/shard_map/ppermute | solution.py:381
  457.5 85.8 %all-to-all-start.3 = ((bf16[4,2,256,576]{2,3,1,0:T(8,128)(2,1)}), bf16[4,2,256,576]{2,3,1,0:T(8,128)(2,1)S(1)}, u32[]{:S(2)}, u32[]{:S(2)}) async-start(bf16[4,2,256,576]{2,3,1,0:T(8,128)(2,1)} %copy.157), calls=%async_computation.4 | async-start | bytes 4718592 | tf_op jit(solution)/shard_map/all_to_all | solution.py:327
  663.5 17.8 %collective-permute-start.16 = (bf16[2,256,768]{2,1,0:T(8,128)(2,1)}, bf16[2,256,768]{2,1,0:T(8,128)(2,1)S(1)}, u32[]{:S(2)}, u32[]{:S(2)}) collective-permute-start(bf16[2,256,768]{2,1,0:T(8,128)(2,1)} %broadcast_select_fusion.5), channel_id=1, source_target_pairs={{0,16},{4,20},{8,24},{12,28},{16,0},{20,4},{24,8},{28,12},{1,17},{... | collective-permute-start | bytes 2359304 | tf_op jit(solution)/shard_map/ppermute | solution.py:338
  664.9 17.5 %collective-permute-start.17 = (bf16[2,256,768]{2,1,0:T(8,128)(2,1)}, bf16[2,256,768]{2,1,0:T(8,128)(2,1)}, u32[]{:S(2)}, u32[]{:S(2)}) collective-permute-start(bf16[2,256,768]{2,1,0:T(8,128)(2,1)} %broadcast_select_fusion.9), channel_id=1, source_target_pairs={{0,8},{4,12},{8,0},{12,4},{16,24},{20,28},{24,16},{28,20},{1,9},{5... | collective-permute-start | bytes 2359304 | tf_op jit(solution)/shard_map/ppermute | solution.py:338
  (81 other events, 806.5 us)
Sparse Core Ops, SparseCore 0:
  14.1 60.1 all-gather.7
  76.2 90.4 all-gather.9
  168.6 83.6 all-gather.5
  290.6 100.8 reduce-scatter.3
  394.6 42.3 reduce-scatter.7
  440.4 53.7 reduce-scatter.5

commit v2 on v0

--- a/solution.py
+++ b/solution.py
@@ -372,15 +372,20 @@
     return low, high
 
 
-LINE = ([(0, 1), (3, 2)], [(1, 2), (2, 1)], [(1, 0), (2, 3)])
+LINE = ([(0, 1), (3, 2)], [(1, 2), (2, 1)])
 
 
 def line_sum(value, step):
     if lax.axis_size("seq") != 4:
         return lax.psum(value, "seq") if step == 0 else value
     other = lax.ppermute(value, "seq", LINE[step])
-    if step < 2:
-        return value + other
+    return value + other
+
+
+def line_back(value):
+    if lax.axis_size("seq") != 4:
+        return value
+    other = lax.ppermute(value, "seq", [(1, 0), (2, 3)])
     return jnp.where((lax.axis_index("seq") % 3) == 0, other, value)
 
 
@@ -808,7 +813,8 @@
         vectors.append(part.reshape(many, size).T if matrix else part)
         at += many * size
     bigs = [piece.astype(F32) for piece in outs[: len(big)]]
-    return bigs, [piece.astype(F32) for piece in outs[len(big) + 1 :]], vectors
+    early = [piece.astype(F32) for piece in outs[len(big) + 1 :]]
+    return bigs, early, vectors
 
 
 def scatter_sum(grad):
@@ -948,9 +954,8 @@
     d_context = d_context.reshape(seqs, local, parts, per * HEAD).transpose(2, 0, 1, 3)
     d_project = attention_backward(qkv, exchange(d_context), own_lengths, per)
     sum_conv, d_char_state, d_project = lax.optimization_barrier((sum_conv, d_char_state, d_project))
+    sum_conv = line_sum(sum_conv, 0)
     d_project = exchange(d_project)
-    sum_conv = line_sum(sum_conv, 0)
-    d_project = d_project.transpose(1, 2, 0, 3).reshape(rows, 3 * width)
 
     d_gates, grad_gru_h, grad_gru_bias = gru_backward(
         counts, row_chars, gru_x, gru_h, gru_bias, d_char_state
@@ -960,8 +965,9 @@
     d_gates = d_gates.reshape(NCHAR * rows, 2 * three)
     grad_gru_x = dot_left(flat_chars, d_gates)
     chars_back = dot_right(d_gates, gru_x).astype(BF)
-    chars_back, sum_conv = lax.optimization_barrier((chars_back, sum_conv))
+    chars_back, d_project = lax.optimization_barrier((chars_back, d_project))
     chars_back = chars_back.reshape(NCHAR, seqs, local, width).transpose(1, 2, 0, 3)
+    d_project = d_project.transpose(1, 2, 0, 3).reshape(rows, 3 * width)
 
     grad_qkv = dot_left(flat_tokens, d_project)
     sums = heads_last(column_sum(d_project)[None], parts)[0]
@@ -987,7 +993,7 @@
     outs = relocate_last(masks, outs, 2, big[-1])
     g_in, g_qkv, g_gru_x, g_gru_h, g_out = big
     g_back, g_blend = early
-    g_conv = line_sum(sum_conv, 2).astype(F32)
+    g_conv = line_back(sum_conv).astype(F32)
     g_b_qv, g_b_in, g_gru_bias, g_conv_b, g_gain, g_shift, g_rows = small
     return (
         outs[0],

time: 700 us -> 672 us (0.960)
  waiting for transfers between devices: 130 us -> 97.8 us
    ppermute x3 -> x2, waiting for transfers between devices: 39.7 us -> 0.01 us  [line_sum(): other = lax.ppermute(value, 'seq', LINE[step])]
  transfers between devices with their start and end apart: 29 -> 29, of which waited for: 9 -> 11; matrix products, arithmetic and copies ran while one was open for 37% -> 38% of each run, Pallas kernels for 30% -> 32%
where the time goes in v2:
time: 672 us; the launch traced here: 664 us
  Pallas kernels  209 us (31%)
  matrix products  121 us (18%)
  local copies, waits for them, and re-layouts  103 us (15%)
  waiting for transfers between devices  97.8 us (15%)
  other arithmetic  74.5 us (11%)
  starting transfers between devices  43.6 us (6%)
  between operations  15.5 us (2%)
    pallas_call x1, Pallas kernels, sum_grads(): pl.pallas_call(partial(sum_kernel, spans, pre_spans, late, pre, high, lag...  95.4 us
    dot_general x10, matrix products, dot_right(): lax.dot_general(left, right, (((1,), (1,)), ((), ())), preferred_element_...  50.5 us
    all_gather x2, waiting for transfers between devices, pack(): return lax.all_gather(jnp.concatenate(pieces, axis=0), 'dp', axis=0)  46.2 us
    pallas_call x1, Pallas kernels, attention_backward(): pl.pallas_call(partial(attention_backward_kernel, per), grid_spec=pltpu.P...  37.4 us
    dot_general x8, matrix products, dot_left(): lax.dot_general(left, right, (((0,), (0,)), ((), ())), preferred_element_...  37.4 us
    pallas_call x1, Pallas kernels, gru_backward(): pl.pallas_call(gru_backward_kernel, grid=(rows // high,), in_specs=gru_sp...  36.7 us
    all_to_all x4, waiting for transfers between devices, exchange(): return lax.all_to_all(blocks, 'seq', split_axis=0, concat_axis=0)  33.3 us
    dot_general x7, matrix products, dot_plain(): return jnp.dot(left, right, preferred_element_type=F32)  32.9 us
  transfers between devices with their start and end apart: 29, of which 11 were waited for; matrix products, arithmetic and copies ran while one was open for 38% of the time, Pallas kernels for 32%

profile of v2, /device:TPU:0, one launch (start us, length us, event | category | flops | bytes accessed | tf_op | source)
XLA Modules:
  0.0 664.4 jit_solution(9272562704850969800)
XLA Ops:
  28.1 46.2 %all-gather.8.cloned.1.call-done = bf16[1984,2304]{1,0:T(8,128)(2,1)} async-done(((bf16[248,2304]{1,0:T(8,128)(2,1)}), bf16[1984,2304]{1,0:T(8,128)(2,1)}) %all-gather.8.cloned.1.call-update) | async-done | bytes 9142288 | tf_op jit(solution)/shard_map/all_gather | solution.py:754
  75.4 5.4 fusion.68
  84.5 4.9 fusion.11
  89.4 5.0 reshape.453
  96.1 4.9 all-to-all-start
  112.1 20.1 %gru_forward.1 = f32[512,768]{1,0:T(8,128)} custom-call(s32[512,1]{1,0:T(8,128)} %bitcast.257, bf16[4,512,768]{2,1,0:T(8,128)(2,1)} %bitcast.225, bf16[768,2304]{1,0:T(8,128)(2,1)} %bitcast.220, bf16[384,2304]{1,0:T(8,128)(2,1)} %bitcast.241, f32[2,2304]{1,0:T(2,128)} %reshape.456.bias_ref), custom_call_target="tpu_custom_call" | custom-call | flops 10871635968 | bytes 10000000 | tf_op jit(solution)/shard_map/gru_forward/pallas_call | solution.py:104
  132.2 23.1 %all-to-all-done = bf16[4,2,256,576]{2,3,1,0:T(8,128)(2,1)S(1)} async-done(((bf16[4,2,256,576]{2,3,1,0:T(8,128)(2,1)}), bf16[4,2,256,576]{2,3,1,0:T(8,128)(2,1)S(1)}, u32[]{:S(2)}, u32[]{:S(2)}) %all-to-all-start) | async-done | bytes 2359328 | tf_op jit(solution)/shard_map/all_to_all | solution.py:327
  157.8 19.7 %attend_forward.1 = bf16[4,2,256,192]{3,2,1,0:T(8,128)(2,1)} custom-call(s32[2]{0:T(128)} %dynamic_slice.3.len_ref, bf16[4,2,256,576]{3,2,1,0:T(8,128)(2,1)} %copy.145.qkv_ref), custom_call_target="tpu_custom_call" | custom-call | tf_op jit(solution)/shard_map/attend_forward/pallas_call | solution.py:249
  191.0 6.7 %fusion.67 = (bf16[8,384,768]{2,1,0:T(8,128)(2,1)}, bf16[8,384,768]{2,1,0:T(8,128)(2,1)S(1)}) fusion(bf16[8,1064,768]{2,1,0:T(8,128)(2,1)} %bitcast.196), kind=kLoop, calls=%fused_computation.193 | loop fusion | bytes 18874368 | tf_op jit(solution)/shard_map/slice | solution.py:763
  215.7 7.3 %fusion.3 = (f32[512,3072]{1,0:T(8,128)}, bf16[512,3072]{1,0:T(8,128)(2,1)S(1)}) fusion(f32[3072]{0:T(1024)S(1)} %add.232, bf16[768,3072]{1,0:T(8,128)(2,1)S(1)} %bitcast.211, f32[512,768]{1,0:T(8,128)S(1)} %get-tuple-element.236, f32[768]{0:T(1024)S(1)} %add.229, f32[768]{0:T(1024)S(1)} %mul.297, f32[512]{0:T(512)S(1)} %add_rsqrt_fusion.3, ...), kind=kOutput, calls=%fused_computation.5 | convolution fusion | flops 2435186688 | bytes 15751168 | tf_op jit(solution)/shard_map/dot_general | solution.py:19
  243.4 9.1 %all-gather.6.cloned.1.call-done = bf16[4608,1536]{1,0:T(8,128)(2,1)} async-done(((bf16[576,1536]{1,0:T(8,128)(2,1)}), bf16[4608,1536]{1,0:T(8,128)(2,1)}) %all-gather.6.cloned.1.call-update) | async-done | bytes 14155792 | tf_op jit(solution)/shard_map/all_gather | solution.py:861
  252.5 14.4 %fusion.21 = (f32[512,1536]{1,0:T(8,128)S(1)}, f32[512,1536]{1,0:T(8,128)S(1)}) fusion(f32[1536]{0:T(1024)S(1)} %add.252, bf16[4608,1536]{1,0:T(8,128)(2,1)} %all-gather.6.cloned.1.call-done, bf16[512,1536]{1,0:T(8,128)(2,1)} %bitcast.246, bf16[512,1536]{1,0:T(8,128)(2,1)S(1)} %bitcast.191, bf16[512,1536]{1,0:T(8,128)(2,1)} %bitcast.244), kind=kOutput, calls=%fused_computation.31 | convolution fusion | flops 7269777408 | bytes 25171968 | tf_op jit(solution)/shard_map/dot_general | solution.py:19
  279.8 10.9 %convolution_convert_fusion = bf16[4608,1536]{1,0:T(8,128)(2,1)} fusion(bf16[512,1536]{1,0:T(8,128)(2,1)S(1)} %fusion.22, bf16[512,1536]{1,0:T(8,128)(2,1)S(1)} %bitcast.247, bf16[512,1536]{1,0:T(8,128)(2,1)S(1)} %bitcast.192, bf16[512,1536]{1,0:T(8,128)(2,1)S(1)} %bitcast.245), kind=kOutput, calls=%fused_computation | convolution fusion | flops 7268990976 | bytes 20447232 | tf_op jit(solution)/shard_map/dot_general | solution.py:23
  306.5 5.1 fusion.6
  338.8 7.9 %fusion.80 = (bf16[3072]{0:T(1024)(128)(2,1)S(1)}, bf16[512,3072]{1,0:T(8,128)(2,1)}) fusion(f32[512,3072]{1,0:T(8,128)} %get-tuple-element.122, bf16[512,768]{1,0:T(8,128)(2,1)S(1)} %get-tuple-element.121, bf16[3072,768]{1,0:T(8,128)(2,1)} %bitcast.213), kind=kOutput, calls=%fused_computation.206 | convolution fusion | flops 2420634624 | bytes 14948352 | tf_op jit(solution)/shard_map/dot_general | solution.py:27
  346.8 7.9 %multiply_reduce_fusion.1 = (bf16[768]{0:T(1024)(128)(2,1)S(1)}, f32[512]{0:T(512)S(1)}, f32[512]{0:T(512)S(1)}, bf16[768]{0:T(1024)(128)(2,1)S(1)}, f32[512,768]{1,0:T(8,128)}) fusion(f32[512,768]{1,0:T(8,128)S(1)} %copy-done.8, f32[512]{0:T(512)S(1)} %add_rsqrt_fusion.3, f32[512]{0:T(512)S(1)} %broadcast_multiply_fusion.9, f32[768]{0:T(1024)S(1)} %mul.297, ...), kind=kOutput, calls=%fused_computation.66 | convolution fusion | flops 2419848704 | bytes 12597248 | tf_op jit(solution)/shard_map/dot_general | solution.py:27
  380.6 8.7 %all-to-all-done.2 = bf16[4,2,256,192]{2,3,1,0:T(8,128)(2,1)S(1)} async-done(((bf16[4,2,256,192]{2,3,1,0:T(8,128)(2,1)}), bf16[4,2,256,192]{2,3,1,0:T(8,128)(2,1)S(1)}, u32[]{:S(2)}, u32[]{:S(2)}) %all-to-all-start.2) | async-done | bytes 786464 | tf_op jit(solution)/shard_map/all_to_all | solution.py:327
  390.5 37.4 %attend_backward.1 = bf16[4,2,256,576]{3,2,1,0:T(8,128)(2,1)} custom-call(s32[2]{0:T(128)} %dynamic_slice.3.len_ref, bf16[4,2,256,576]{3,2,1,0:T(8,128)(2,1)} %copy.145.qkv_ref, bf16[4,2,256,192]{3,2,1,0:T(8,128)(2,1)} %copy.155.grad_ref), custom_call_target="tpu_custom_call" | custom-call | tf_op jit(solution)/shard_map/attend_backward/pallas_call | solution.py:306
  438.5 36.7 %gru_backward.1 = (bf16[4,512,2304]{2,1,0:T(8,128)(2,1)}, bf16[384,2304]{1,0:T(8,128)(2,1)}, f32[2,2304]{1,0:T(2,128)}) custom-call(s32[512,1]{1,0:T(8,128)} %bitcast.258, bf16[4,512,768]{2,1,0:T(8,128)(2,1)} %bitcast.226, bf16[768,2304]{1,0:T(8,128)(2,1)} %bitcast.221, bf16[384,2304]{1,0:T(8,128)(2,1)} %bitcast.242, f32[2,2304]{1,0:T(2,128)} %reshape.456.bias_ref, ...), custom_call_target="tpu_custom_call" | custom-call | flops 18119393280 | bytes 30000000 | tf_op jit(solution)/shard_map/gru_backward/pallas_call | solution.py:195
  482.2 11.4 %convolution_convert_fusion.5 = bf16[2048,768]{1,0:T(8,128)(2,1)} fusion(bf16[2048,2304]{1,0:T(8,128)(2,1)} %bitcast.281, bf16[768,2304]{1,0:T(8,128)(2,1)S(1)} %bitcast.222), kind=kOutput, calls=%fused_computation.24 | convolution fusion | flops 7249330176 | bytes 16121856 | tf_op jit(solution)/shard_map/dot_general | solution.py:27
  493.6 9.8 %convolution_convert_fusion.1 = bf16[2304,768]{0,1:T(8,128)(2,1)} fusion(bf16[2048,2304]{1,0:T(8,128)(2,1)S(1)} %bitcast.284, bf16[2048,768]{1,0:T(8,128)(2,1)S(1)} %bitcast.227), kind=kOutput, calls=%fused_computation.9 | convolution fusion | flops 7249526784 | bytes 16121856 | tf_op jit(solution)/shard_map/dot_general | solution.py:23
  514.9 95.4 %sum_grads.1 = (bf16[96,3072]{1,0:T(8,128)(2,1)}, bf16[96,2304]{1,0:T(8,128)(2,1)}, bf16[96,2304]{1,0:T(8,128)(2,1)}, bf16[48,2304]{1,0:T(8,128)(2,1)}, bf16[96,...) custom-call(bf16[4,2,96,3072]{3,2,1,0:T(8,128)(2,1)} %bitcast.217, ...), custom_call_target="tpu_custom_call" | custom-call | tf_op jit(solution)/shard_map/sum_grads/pallas_call | solution.py:696
  615.7 6.0 copy.181
  648.7 5.1 collective-permute-done.18
  (415 shorter events, 239.7 us)
Async XLA Ops:
  7.2 67.1 %all-gather.8.cloned.1.call-start = ((), (), s32[]{:S(2)}) async-start(), calls=%async_computation.11 | async-start | bytes 10285056 | tf_op jit(solution)/shard_map/all_gather | solution.py:754
  14.0 163.5 %all-gather.10.cloned.1.call-start = ((), (), s32[]{:S(2)}) async-start(), calls=%async_computation.12 | async-start | bytes 14708736 | tf_op jit(solution)/shard_map/all_gather | solution.py:754
  21.7 230.8 %all-gather.6.cloned.1.call-start = ((), (), s32[]{:S(2)}) async-start(), calls=%async_computation.7 | async-start | bytes 15925248 | tf_op jit(solution)/shard_map/all_gather | solution.py:861
  23.2 66.2 %collective-permute-start = (bf16[2,256,768]{2,1,0:T(8,128)(2,1)}, bf16[2,256,768]{2,1,0:T(8,128)(2,1)}, u32[]{:S(2)}, u32[]{:S(2)}) collective-permute-start(bf16[2,256,768]{2,1,0:T(8,128)(2,1)} %param.27), channel_id=1, source_target_pairs={{0,4},{4,0},{8,12},{12,8},{16,20},{20,16},{24,28},{28,24},{1,5},{5... | collective-permute-start | bytes 2359304 | tf_op jit(solution)/shard_map/ppermute | solution.py:338
  23.7 65.7 %collective-permute-start.1 = (bf16[2,256,768]{2,1,0:T(8,128)(2,1)}, bf16[2,256,768]{2,1,0:T(8,128)(2,1)}, u32[]{:S(2)}, u32[]{:S(2)}) collective-permute-start(bf16[2,256,768]{2,1,0:T(8,128)(2,1)} %param.28), channel_id=1, source_target_pairs={{0,4},{4,0},{8,12},{12,8},{16,20},{20,16},{24,28},{28,24},{1,5},{5... | collective-permute-start | bytes 2359304 | tf_op jit(solution)/shard_map/ppermute | solution.py:338
  96.1 59.1 %all-to-all-start = ((bf16[4,2,256,576]{2,3,1,0:T(8,128)(2,1)}), bf16[4,2,256,576]{2,3,1,0:T(8,128)(2,1)S(1)}, u32[]{:S(2)}, u32[]{:S(2)}) async-start(bf16[4,2,256,576]{2,3,1,0:T(8,128)(2,1)} %copy.142), calls=%async_computation | async-start | bytes 4718592 | tf_op jit(solution)/shard_map/all_to_all | solution.py:327
  110.0 102.8 %collective-permute-start.3 = (bf16[2,256,768]{2,1,0:T(8,128)(2,1)S(1)}, bf16[2,256,768]{2,1,0:T(8,128)(2,1)}, u32[]{:S(2)}, u32[]{:S(2)}) collective-permute-start(bf16[2,256,768]{2,1,0:T(8,128)(2,1)S(1)} %get-tuple-element.103), channel_id=1, source_target_pairs={{0,16},{4,20},{8,24},{12,28},{16,0},{20,4},{24,8},{28,12},{1,17},{... | collective-permute-start | bytes 2359304 | tf_op jit(solution)/shard_map/ppermute | solution.py:338
  111.1 101.7 %collective-permute-start.2 = (bf16[2,256,768]{2,1,0:T(8,128)(2,1)}, bf16[2,256,768]{2,1,0:T(8,128)(2,1)}, u32[]{:S(2)}, u32[]{:S(2)}) collective-permute-start(bf16[2,256,768]{2,1,0:T(8,128)(2,1)} %get-tuple-element.101), channel_id=1, source_target_pairs={{0,8},{4,12},{8,0},{12,4},{16,24},{20,28},{24,16},{28,20},{1,9},{5... | collective-permute-start | bytes 2359304 | tf_op jit(solution)/shard_map/ppermute | solution.py:338
  179.8 30.8 %all-to-all-start.1 = ((bf16[4,2,256,192]{2,3,1,0:T(8,128)(2,1)}), bf16[4,2,256,192]{2,3,1,0:T(8,128)(2,1)}, u32[]{:S(2)}, u32[]{:S(2)}) async-start(bf16[4,2,256,192]{2,3,1,0:T(8,128)(2,1)} %copy.146), calls=%async_computation.1 | async-start | bytes 1572864 | tf_op jit(solution)/shard_map/all_to_all | solution.py:327
  184.0 244.0 %reduce-scatter.4.cloned.1.call-start = ((), (), s32[]{:S(2)}) async-start(), calls=%async_computation.8 | async-start | bytes 15925248 | tf_op jit(solution)/shard_map/reduce_scatter | solution.py:821
  237.9 32.8 %collective-permute-start.8 = (bf16[2,256,768]{2,1,0:T(8,128)(2,1)}, bf16[2,256,768]{2,1,0:T(8,128)(2,1)}, u32[]{:S(2)}, u32[]{:S(2)}) collective-permute-start(bf16[2,256,768]{2,1,0:T(8,128)(2,1)} %broadcast_select_fusion.7), channel_id=1, source_target_pairs={{0,16},{4,20},{8,24},{12,28},{16,0},{20,4},{24,8},{28,12},{1,17},{... | collective-permute-start | bytes 2359304 | tf_op jit(solution)/shard_map/ppermute | solution.py:338
  239.2 31.5 %collective-permute-start.9 = (bf16[2,256,768]{2,1,0:T(8,128)(2,1)}, bf16[2,256,768]{2,1,0:T(8,128)(2,1)}, u32[]{:S(2)}, u32[]{:S(2)}) collective-permute-start(bf16[2,256,768]{2,1,0:T(8,128)(2,1)} %broadcast_select_fusion.11), channel_id=1, source_target_pairs={{0,8},{4,12},{8,0},{12,4},{16,24},{20,28},{24,16},{28,20},{1,9},{5... | collective-permute-start | bytes 2359304 | tf_op jit(solution)/shard_map/ppermute | solution.py:338
  290.7 224.2 %reduce-scatter.8.cloned.1.call-start = ((), (), s32[]{:S(2)}) async-start(), calls=%async_computation.10 | async-start | bytes 2654208 | tf_op jit(solution)/shard_map/reduce_scatter | solution.py:821
  295.7 16.4 %collective-permute-start.12 = (bf16[2,1,1536]{2,1,0:T(2,128)(2,1)S(1)}, bf16[2,1,1536]{2,1,0:T(2,128)(2,1)S(1)}, u32[]{:S(2)}, u32[]{:S(2)}) collective-permute-start(bf16[2,1,1536]{2,1,0:T(2,128)(2,1)S(1)} %get-tuple-element.212), channel_id=1, source_target_pairs={{1,0},{2,1},{3,2},{5,4},{6,5},{7,6},{9,8},{10,9},{11,10},{13,12},{... | collective-permute-start | bytes 18440 | tf_op jit(solution)/shard_map/ppermute | solution.py:371
  304.7 58.5 %collective-permute-start.11 = (bf16[2,256,768]{2,1,0:T(8,128)(2,1)}, bf16[2,256,768]{2,1,0:T(8,128)(2,1)}, u32[]{:S(2)}, u32[]{:S(2)}) collective-permute-start(bf16[2,256,768]{2,1,0:T(8,128)(2,1)} %get-tuple-element.126), channel_id=1, source_target_pairs={{0,16},{4,20},{8,24},{12,28},{16,0},{20,4},{24,8},{28,12},{1,17},{... | collective-permute-start | bytes 2359304 | tf_op jit(solution)/shard_map/ppermute | solution.py:338
  305.2 58.0 %collective-permute-start.10 = (bf16[2,256,768]{2,1,0:T(8,128)(2,1)}, bf16[2,256,768]{2,1,0:T(8,128)(2,1)}, u32[]{:S(2)}, u32[]{:S(2)}) collective-permute-start(bf16[2,256,768]{2,1,0:T(8,128)(2,1)} %get-tuple-element.124), channel_id=1, source_target_pairs={{0,8},{4,12},{8,0},{12,4},{16,24},{20,28},{24,16},{28,20},{1,9},{5... | collective-permute-start | bytes 2359304 | tf_op jit(solution)/shard_map/ppermute | solution.py:338
  326.2 188.7 %reduce-scatter.6.cloned.1.call-start = ((), (), s32[]{:S(2)}) async-start(), calls=%async_computation.9 | async-start | bytes 5308416 | tf_op jit(solution)/shard_map/reduce_scatter | solution.py:821
  365.5 23.8 %all-to-all-start.2 = ((bf16[4,2,256,192]{2,3,1,0:T(8,128)(2,1)}), bf16[4,2,256,192]{2,3,1,0:T(8,128)(2,1)S(1)}, u32[]{:S(2)}, u32[]{:S(2)}) async-start(bf16[4,2,256,192]{2,3,1,0:T(8,128)(2,1)} %copy.153), calls=%async_computation.3 | async-start | bytes 1572864 | tf_op jit(solution)/shard_map/all_to_all | solution.py:327
  428.0 48.3 %collective-permute-start.14 = (bf16[576,1536]{1,0:T(8,128)(2,1)}, bf16[576,1536]{1,0:T(8,128)(2,1)}, u32[]{:S(2)}, u32[]{:S(2)}) collective-permute-start(bf16[576,1536]{1,0:T(8,128)(2,1)} %reduce-scatter.4.cloned.1.call-done), channel_id=1, source_target_pairs={{0,1},{3,2},{4,5},{7,6},{8,9},{11,10},{12,13},{15,14},{16,17},{19,... | collective-permute-start | bytes 5308424 | tf_op jit(solution)/shard_map/ppermute | solution.py:381
  434.9 70.1 %all-to-all-start.3 = ((bf16[4,2,256,576]{2,3,1,0:T(8,128)(2,1)}), bf16[4,2,256,576]{2,3,1,0:T(8,128)(2,1)S(1)}, u32[]{:S(2)}, u32[]{:S(2)}) async-start(bf16[4,2,256,576]{2,3,1,0:T(8,128)(2,1)} %copy.157), calls=%async_computation.4 | async-start | bytes 4718592 | tf_op jit(solution)/shard_map/all_to_all | solution.py:327
  480.2 130.2 %collective-permute-start.17 = (bf16[576,1536]{1,0:T(8,128)(2,1)}, bf16[576,1536]{1,0:T(8,128)(2,1)}, u32[]{:S(2)}, u32[]{:S(2)}) collective-permute-start(bf16[576,1536]{1,0:T(8,128)(2,1)} %add.273), channel_id=1, source_target_pairs={{1,2},{2,1},{5,6},{6,5},{9,10},{10,9},{13,14},{14,13},{17,18},{18,... | collective-permute-start | bytes 5308424 | tf_op jit(solution)/shard_map/ppermute | solution.py:381
  612.8 41.0 %collective-permute-start.18 = (bf16[576,1536]{1,0:T(8,128)(2,1)S(1)}, bf16[576,1536]{1,0:T(8,128)(2,1)}, u32[]{:S(2)}, u32[]{:S(2)}) collective-permute-start(bf16[576,1536]{1,0:T(8,128)(2,1)S(1)} %add.276), channel_id=1, source_target_pairs={{1,0},{2,3},{5,4},{6,7},{9,8},{10,11},{13,12},{14,15},{17,16},{18,... | collective-permute-start | bytes 5308424 | tf_op jit(solution)/shard_map/ppermute | solution.py:388
  624.8 18.3 %collective-permute-start.15 = (bf16[2,256,768]{2,1,0:T(8,128)(2,1)}, bf16[2,256,768]{2,1,0:T(8,128)(2,1)}, u32[]{:S(2)}, u32[]{:S(2)}) collective-permute-start(bf16[2,256,768]{2,1,0:T(8,128)(2,1)} %broadcast_select_fusion.5), channel_id=1, source_target_pairs={{0,16},{4,20},{8,24},{12,28},{16,0},{20,4},{24,8},{28,12},{1,17},{... | collective-permute-start | bytes 2359304 | tf_op jit(solution)/shard_map/ppermute | solution.py:338
  626.1 17.9 %collective-permute-start.16 = (bf16[2,256,768]{2,1,0:T(8,128)(2,1)}, bf16[2,256,768]{2,1,0:T(8,128)(2,1)}, u32[]{:S(2)}, u32[]{:S(2)}) collective-permute-start(bf16[2,256,768]{2,1,0:T(8,128)(2,1)} %broadcast_select_fusion.9), channel_id=1, source_target_pairs={{0,8},{4,12},{8,0},{12,4},{16,24},{20,28},{24,16},{28,20},{1,9},{5... | collective-permute-start | bytes 2359304 | tf_op jit(solution)/shard_map/ppermute | solution.py:338
  (72 other events, 395.6 us)
Sparse Core Ops, SparseCore 0:
  14.1 60.1 all-gather.7
  76.2 90.4 all-gather.9
  168.6 83.8 all-gather.5
  290.8 100.8 reduce-scatter.3
  394.9 42.3 reduce-scatter.7
  440.6 53.7 reduce-scatter.5

commit v3 on v2

--- a/solution.py
+++ b/solution.py
@@ -738,10 +738,6 @@
     return jnp.concatenate([piece.T.reshape(-1) for piece in small])
 
 
-def gather_packed(weights, small, wide):
-    return unpack(pack(weights, small, wide), weights, small, wide)
-
-
 def pack(weights, small, wide):
     pieces = []
     for weight in weights:
@@ -854,7 +850,9 @@
     place = lax.axis_index("dp")
     own_lengths = lax.dynamic_slice(lengths, (place * seqs,), (seqs,))
     first = (heads_first(w_qkv, parts), gru_x, gru_h)
-    (w_qkv, gru_x, gru_h), (b_qv, gru_bias) = gather_packed(first, (b_qv, gru_bias), 3 * width)
+    first_small = (b_qv, gru_bias)
+    first_packed = pack(first, first_small, 3 * width)
+    (w_qkv, _, _), (b_qv, _) = unpack(first_packed, first, first_small, 3 * width)
     middle = (w_out, w_in, w_back, blend_w)
     small = (b_in, conv_b, norm_gain, norm_bias, row_bias)
     packed = pack(middle, small, width)
@@ -869,7 +867,8 @@
     project = (dot_plain(flat_tokens, w_qkv) + bias).astype(BF)
     cots = (token_cot, char_cot)
     cots, project = relocate_one(masks, cots, 0, project)
-    project, row_chars = lax.optimization_barrier((project, row_chars))
+    project, row_chars, first_packed = lax.optimization_barrier((project, row_chars, first_packed))
+    (_, gru_x, gru_h), (_, gru_bias) = unpack(first_packed, first, first_small, 3 * width)
     span = 3 * per * HEAD
     qkv = project.reshape(seqs, local, parts, span).transpose(2, 0, 1, 3)
     qkv = exchange(qkv)

time: 672 us -> 676 us (level)
    slice x5 -> x6, local copies, waits for them, and re-layouts: 19.1 us -> 20 us  [unpack(): part = full[:, at:at + blocks * rows].reshape(groups, blocks, rows, wide)]
    unnamed x154 -> x153, local copies, waits for them, and re-layouts: 29 us -> 29.2 us
  transfers between devices with their start and end apart: 29 -> 29, of which waited for: 11 -> 11; matrix products, arithmetic and copies ran while one was open for 38% -> 38% of each run, Pallas kernels for 32% -> 31%
where the time goes in v3:
time: 676 us; the launch traced here: 668 us
  Pallas kernels  209 us (31%)
  matrix products  121 us (18%)
  local copies, waits for them, and re-layouts  104 us (15%)
  waiting for transfers between devices  101 us (15%)
  other arithmetic  74.5 us (11%)
  starting transfers between devices  42.9 us (6%)
  between operations  15.6 us (2%)
    pallas_call x1, Pallas kernels, sum_grads(): pl.pallas_call(partial(sum_kernel, spans, pre_spans, late, pre, high, lag...  95.4 us
    dot_general x10, matrix products, dot_right(): lax.dot_general(left, right, (((1,), (1,)), ((), ())), preferred_element_...  50.4 us
    all_gather x2, waiting for transfers between devices, pack(): return lax.all_gather(jnp.concatenate(pieces, axis=0), 'dp', axis=0)  46.2 us
    pallas_call x1, Pallas kernels, attention_backward(): pl.pallas_call(partial(attention_backward_kernel, per), grid_spec=pltpu.P...  37.4 us
    dot_general x8, matrix products, dot_left(): lax.dot_general(left, right, (((0,), (0,)), ((), ())), preferred_element_...  37.4 us
    pallas_call x1, Pallas kernels, gru_backward(): pl.pallas_call(gru_backward_kernel, grid=(rows // high,), in_specs=gru_sp...  36.7 us
    dot_general x7, matrix products, dot_plain(): return jnp.dot(left, right, preferred_element_type=F32)  32.8 us
    all_to_all x4, waiting for transfers between devices, exchange(): return lax.all_to_all(blocks, 'seq', split_axis=0, concat_axis=0)  29.7 us
  transfers between devices with their start and end apart: 29, of which 11 were waited for; matrix products, arithmetic and copies ran while one was open for 38% of the time, Pallas kernels for 31%

profile of v3, /device:TPU:0, one launch (start us, length us, event | category | flops | bytes accessed | tf_op | source)
XLA Modules:
  0.0 668.0 jit_solution(16364098874382562859)
XLA Ops:
  28.2 46.2 %all-gather.8.cloned.1.call-done = bf16[1984,2304]{1,0:T(8,128)(2,1)} async-done(((bf16[248,2304]{1,0:T(8,128)(2,1)}), bf16[1984,2304]{1,0:T(8,128)(2,1)}) %all-gather.8.cloned.1.call-update) | async-done | bytes 9142288 | tf_op jit(solution)/shard_map/all_gather | solution.py:750
  81.3 4.8 fusion.11
  86.2 5.1 reshape.460
  93.0 4.9 all-to-all-start
  113.2 19.7 %gru_forward.1 = f32[512,768]{1,0:T(8,128)} custom-call(s32[512,1]{1,0:T(8,128)} %bitcast.262, bf16[4,512,768]{2,1,0:T(8,128)(2,1)} %bitcast.230, bf16[768,2304]{1,0:T(8,128)(2,1)} %bitcast.225, bf16[384,2304]{1,0:T(8,128)(2,1)} %bitcast.246, f32[2,2304]{1,0:T(2,128)} %reshape.520.bias_ref), custom_call_target="tpu_custom_call" | custom-call | flops 10871635968 | bytes 10000000 | tf_op jit(solution)/shard_map/gru_forward/pallas_call | solution.py:104
  132.9 19.2 %all-to-all-done = bf16[4,2,256,576]{2,3,1,0:T(8,128)(2,1)S(1)} async-done(((bf16[4,2,256,576]{2,3,1,0:T(8,128)(2,1)}), bf16[4,2,256,576]{2,3,1,0:T(8,128)(2,1)S(1)}, u32[]{:S(2)}, u32[]{:S(2)}) %all-to-all-start) | async-done | bytes 2359328 | tf_op jit(solution)/shard_map/all_to_all | solution.py:327
  154.7 19.7 %attend_forward.1 = bf16[4,2,256,192]{3,2,1,0:T(8,128)(2,1)} custom-call(s32[2]{0:T(128)} %dynamic_slice.3.len_ref, bf16[4,2,256,576]{3,2,1,0:T(8,128)(2,1)} %copy.145.qkv_ref), custom_call_target="tpu_custom_call" | custom-call | tf_op jit(solution)/shard_map/attend_forward/pallas_call | solution.py:249
  188.0 6.7 %fusion.67 = (bf16[8,384,768]{2,1,0:T(8,128)(2,1)}, bf16[8,384,768]{2,1,0:T(8,128)(2,1)S(1)}) fusion(bf16[8,1064,768]{2,1,0:T(8,128)(2,1)} %bitcast.199), kind=kLoop, calls=%fused_computation.195 | loop fusion | bytes 18874368 | tf_op jit(solution)/shard_map/slice | solution.py:759
  212.9 7.3 %fusion.3 = (f32[512,3072]{1,0:T(8,128)}, bf16[512,3072]{1,0:T(8,128)(2,1)S(1)}) fusion(f32[3072]{0:T(1024)S(1)} %add.232, bf16[768,3072]{1,0:T(8,128)(2,1)S(1)} %bitcast.216, f32[512,768]{1,0:T(8,128)S(1)} %get-tuple-element.236, f32[768]{0:T(1024)S(1)} %add.229, f32[768]{0:T(1024)S(1)} %mul.297, f32[512]{0:T(512)S(1)} %add_rsqrt_fusion.3, ...), kind=kOutput, calls=%fused_computation.5 | convolution fusion | flops 2435186688 | bytes 15751168 | tf_op jit(solution)/shard_map/dot_general | solution.py:19
  240.7 15.4 %all-gather.6.cloned.1.call-done = bf16[4608,1536]{1,0:T(8,128)(2,1)} async-done(((bf16[576,1536]{1,0:T(8,128)(2,1)}), bf16[4608,1536]{1,0:T(8,128)(2,1)}) %all-gather.6.cloned.1.call-update) | async-done | bytes 14155792 | tf_op jit(solution)/shard_map/all_gather | solution.py:859
  256.0 14.4 %fusion.21 = (f32[512,1536]{1,0:T(8,128)S(1)}, f32[512,1536]{1,0:T(8,128)S(1)}) fusion(f32[1536]{0:T(1024)S(1)} %add.252, bf16[4608,1536]{1,0:T(8,128)(2,1)} %all-gather.6.cloned.1.call-done, bf16[512,1536]{1,0:T(8,128)(2,1)} %bitcast.251, bf16[512,1536]{1,0:T(8,128)(2,1)S(1)} %bitcast.194, bf16[512,1536]{1,0:T(8,128)(2,1)} %bitcast.249), kind=kOutput, calls=%fused_computation.31 | convolution fusion | flops 7269777408 | bytes 25171968 | tf_op jit(solution)/shard_map/dot_general | solution.py:19
  283.3 10.9 %convolution_convert_fusion = bf16[4608,1536]{1,0:T(8,128)(2,1)} fusion(bf16[512,1536]{1,0:T(8,128)(2,1)S(1)} %fusion.22, bf16[512,1536]{1,0:T(8,128)(2,1)S(1)} %bitcast.252, bf16[512,1536]{1,0:T(8,128)(2,1)S(1)} %bitcast.195, bf16[512,1536]{1,0:T(8,128)(2,1)S(1)} %bitcast.250), kind=kOutput, calls=%fused_computation | convolution fusion | flops 7268990976 | bytes 20447232 | tf_op jit(solution)/shard_map/dot_general | solution.py:23
  310.3 5.2 fusion.6
  342.8 7.9 %fusion.79 = (bf16[3072]{0:T(1024)(128)(2,1)S(1)}, bf16[512,3072]{1,0:T(8,128)(2,1)}) fusion(f32[512,3072]{1,0:T(8,128)} %get-tuple-element.124, bf16[512,768]{1,0:T(8,128)(2,1)S(1)} %get-tuple-element.123, bf16[3072,768]{1,0:T(8,128)(2,1)} %bitcast.218), kind=kOutput, calls=%fused_computation.207 | convolution fusion | flops 2420634624 | bytes 14948352 | tf_op jit(solution)/shard_map/dot_general | solution.py:27
  350.8 7.9 %multiply_reduce_fusion.1 = (bf16[768]{0:T(1024)(128)(2,1)S(1)}, f32[512]{0:T(512)S(1)}, f32[512]{0:T(512)S(1)}, bf16[768]{0:T(1024)(128)(2,1)S(1)}, f32[512,768]{1,0:T(8,128)}) fusion(f32[512,768]{1,0:T(8,128)S(1)} %copy-done.8, f32[512]{0:T(512)S(1)} %add_rsqrt_fusion.3, f32[512]{0:T(512)S(1)} %broadcast_multiply_fusion.9, f32[768]{0:T(1024)S(1)} %mul.297, ...), kind=kOutput, calls=%fused_computation.66 | convolution fusion | flops 2419848704 | bytes 12597248 | tf_op jit(solution)/shard_map/dot_general | solution.py:27
  362.3 4.9 convolution_convert_fusion.3
  384.4 8.7 %all-to-all-done.2 = bf16[4,2,256,192]{2,3,1,0:T(8,128)(2,1)S(1)} async-done(((bf16[4,2,256,192]{2,3,1,0:T(8,128)(2,1)}), bf16[4,2,256,192]{2,3,1,0:T(8,128)(2,1)S(1)}, u32[]{:S(2)}, u32[]{:S(2)}) %all-to-all-start.2) | async-done | bytes 786464 | tf_op jit(solution)/shard_map/all_to_all | solution.py:327
  394.4 37.4 %attend_backward.1 = bf16[4,2,256,576]{3,2,1,0:T(8,128)(2,1)} custom-call(s32[2]{0:T(128)} %dynamic_slice.3.len_ref, bf16[4,2,256,576]{3,2,1,0:T(8,128)(2,1)} %copy.145.qkv_ref, bf16[4,2,256,192]{3,2,1,0:T(8,128)(2,1)} %copy.155.grad_ref), custom_call_target="tpu_custom_call" | custom-call | tf_op jit(solution)/shard_map/attend_backward/pallas_call | solution.py:306
  442.3 36.7 %gru_backward.1 = (bf16[4,512,2304]{2,1,0:T(8,128)(2,1)}, bf16[384,2304]{1,0:T(8,128)(2,1)}, f32[2,2304]{1,0:T(2,128)}) custom-call(s32[512,1]{1,0:T(8,128)} %bitcast.263, bf16[4,512,768]{2,1,0:T(8,128)(2,1)} %bitcast.231, bf16[768,2304]{1,0:T(8,128)(2,1)} %bitcast.226, bf16[384,2304]{1,0:T(8,128)(2,1)} %bitcast.247, f32[2,2304]{1,0:T(2,128)} %reshape.520.bias_ref, ...), custom_call_target="tpu_custom_call" | custom-call | flops 18119393280 | bytes 30000000 | tf_op jit(solution)/shard_map/gru_backward/pallas_call | solution.py:195
  485.8 11.5 %convolution_convert_fusion.5 = bf16[2048,768]{1,0:T(8,128)(2,1)} fusion(bf16[2048,2304]{1,0:T(8,128)(2,1)} %bitcast.286, bf16[768,2304]{1,0:T(8,128)(2,1)S(1)} %bitcast.227), kind=kOutput, calls=%fused_computation.24 | convolution fusion | flops 7249330176 | bytes 16121856 | tf_op jit(solution)/shard_map/dot_general | solution.py:27
  497.3 9.7 %convolution_convert_fusion.1 = bf16[2304,768]{0,1:T(8,128)(2,1)} fusion(bf16[2048,2304]{1,0:T(8,128)(2,1)S(1)} %bitcast.289, bf16[2048,768]{1,0:T(8,128)(2,1)S(1)} %bitcast.232), kind=kOutput, calls=%fused_computation.9 | convolution fusion | flops 7249526784 | bytes 16121856 | tf_op jit(solution)/shard_map/dot_general | solution.py:23
  518.7 95.4 %sum_grads.1 = (bf16[96,3072]{1,0:T(8,128)(2,1)}, bf16[96,2304]{1,0:T(8,128)(2,1)}, bf16[96,2304]{1,0:T(8,128)(2,1)}, bf16[48,2304]{1,0:T(8,128)(2,1)}, bf16[96,...) custom-call(bf16[4,2,96,3072]{3,2,1,0:T(8,128)(2,1)} %bitcast.222, ...), custom_call_target="tpu_custom_call" | custom-call | tf_op jit(solution)/shard_map/sum_grads/pallas_call | solution.py:696
  619.4 6.0 copy.183
  652.3 5.2 collective-permute-done.18
  (416 shorter events, 241.7 us)
Async XLA Ops:
  7.2 67.1 %all-gather.8.cloned.1.call-start = ((), (), s32[]{:S(2)}) async-start(), calls=%async_computation.11 | async-start | bytes 10285056 | tf_op jit(solution)/shard_map/all_gather | solution.py:750
  14.0 160.4 %all-gather.10.cloned.1.call-start = ((), (), s32[]{:S(2)}) async-start(), calls=%async_computation.12 | async-start | bytes 14708736 | tf_op jit(solution)/shard_map/all_gather | solution.py:750
  21.7 234.3 %all-gather.6.cloned.1.call-start = ((), (), s32[]{:S(2)}) async-start(), calls=%async_computation.7 | async-start | bytes 15925248 | tf_op jit(solution)/shard_map/all_gather | solution.py:859
  23.2 62.9 %collective-permute-start = (bf16[2,256,768]{2,1,0:T(8,128)(2,1)}, bf16[2,256,768]{2,1,0:T(8,128)(2,1)}, u32[]{:S(2)}, u32[]{:S(2)}) collective-permute-start(bf16[2,256,768]{2,1,0:T(8,128)(2,1)} %param.27), channel_id=1, source_target_pairs={{0,4},{4,0},{8,12},{12,8},{16,20},{20,16},{24,28},{28,24},{1,5},{5... | collective-permute-start | bytes 2359304 | tf_op jit(solution)/shard_map/ppermute | solution.py:338
  23.8 62.4 %collective-permute-start.1 = (bf16[2,256,768]{2,1,0:T(8,128)(2,1)}, bf16[2,256,768]{2,1,0:T(8,128)(2,1)}, u32[]{:S(2)}, u32[]{:S(2)}) collective-permute-start(bf16[2,256,768]{2,1,0:T(8,128)(2,1)} %param.28), channel_id=1, source_target_pairs={{0,4},{4,0},{8,12},{12,8},{16,20},{20,16},{24,28},{28,24},{1,5},{5... | collective-permute-start | bytes 2359304 | tf_op jit(solution)/shard_map/ppermute | solution.py:338
  93.0 59.1 %all-to-all-start = ((bf16[4,2,256,576]{2,3,1,0:T(8,128)(2,1)}), bf16[4,2,256,576]{2,3,1,0:T(8,128)(2,1)S(1)}, u32[]{:S(2)}, u32[]{:S(2)}) async-start(bf16[4,2,256,576]{2,3,1,0:T(8,128)(2,1)} %copy.142), calls=%async_computation | async-start | bytes 4718592 | tf_op jit(solution)/shard_map/all_to_all | solution.py:327
  111.2 98.8 %collective-permute-start.3 = (bf16[2,256,768]{2,1,0:T(8,128)(2,1)S(1)}, bf16[2,256,768]{2,1,0:T(8,128)(2,1)}, u32[]{:S(2)}, u32[]{:S(2)}) collective-permute-start(bf16[2,256,768]{2,1,0:T(8,128)(2,1)S(1)} %get-tuple-element.105), channel_id=1, source_target_pairs={{0,16},{4,20},{8,24},{12,28},{16,0},{20,4},{24,8},{28,12},{1,17},{... | collective-permute-start | bytes 2359304 | tf_op jit(solution)/shard_map/ppermute | solution.py:338
  112.2 97.9 %collective-permute-start.2 = (bf16[2,256,768]{2,1,0:T(8,128)(2,1)}, bf16[2,256,768]{2,1,0:T(8,128)(2,1)}, u32[]{:S(2)}, u32[]{:S(2)}) collective-permute-start(bf16[2,256,768]{2,1,0:T(8,128)(2,1)} %get-tuple-element.103), channel_id=1, source_target_pairs={{0,8},{4,12},{8,0},{12,4},{16,24},{20,28},{24,16},{28,20},{1,9},{5... | collective-permute-start | bytes 2359304 | tf_op jit(solution)/shard_map/ppermute | solution.py:338
  176.7 30.8 %all-to-all-start.1 = ((bf16[4,2,256,192]{2,3,1,0:T(8,128)(2,1)}), bf16[4,2,256,192]{2,3,1,0:T(8,128)(2,1)}, u32[]{:S(2)}, u32[]{:S(2)}) async-start(bf16[4,2,256,192]{2,3,1,0:T(8,128)(2,1)} %copy.146), calls=%async_computation.1 | async-start | bytes 1572864 | tf_op jit(solution)/shard_map/all_to_all | solution.py:327
  181.0 250.8 %reduce-scatter.4.cloned.1.call-start = ((), (), s32[]{:S(2)}) async-start(), calls=%async_computation.8 | async-start | bytes 15925248 | tf_op jit(solution)/shard_map/reduce_scatter | solution.py:817
  235.1 39.1 %collective-permute-start.8 = (bf16[2,256,768]{2,1,0:T(8,128)(2,1)}, bf16[2,256,768]{2,1,0:T(8,128)(2,1)}, u32[]{:S(2)}, u32[]{:S(2)}) collective-permute-start(bf16[2,256,768]{2,1,0:T(8,128)(2,1)} %broadcast_select_fusion.7), channel_id=1, source_target_pairs={{0,16},{4,20},{8,24},{12,28},{16,0},{20,4},{24,8},{28,12},{1,17},{... | collective-permute-start | bytes 2359304 | tf_op jit(solution)/shard_map/ppermute | solution.py:338
  236.1 38.1 %collective-permute-start.9 = (bf16[2,256,768]{2,1,0:T(8,128)(2,1)}, bf16[2,256,768]{2,1,0:T(8,128)(2,1)}, u32[]{:S(2)}, u32[]{:S(2)}) collective-permute-start(bf16[2,256,768]{2,1,0:T(8,128)(2,1)} %broadcast_select_fusion.11), channel_id=1, source_target_pairs={{0,8},{4,12},{8,0},{12,4},{16,24},{20,28},{24,16},{28,20},{1,9},{5... | collective-permute-start | bytes 2359304 | tf_op jit(solution)/shard_map/ppermute | solution.py:338
  294.2 224.5 %reduce-scatter.8.cloned.1.call-start = ((), (), s32[]{:S(2)}) async-start(), calls=%async_computation.10 | async-start | bytes 2654208 | tf_op jit(solution)/shard_map/reduce_scatter | solution.py:817
  299.2 16.7 %collective-permute-start.12 = (bf16[2,1,1536]{2,1,0:T(2,128)(2,1)S(1)}, bf16[2,1,1536]{2,1,0:T(2,128)(2,1)S(1)}, u32[]{:S(2)}, u32[]{:S(2)}) collective-permute-start(bf16[2,1,1536]{2,1,0:T(2,128)(2,1)S(1)} %get-tuple-element.212), channel_id=1, source_target_pairs={{1,0},{2,1},{3,2},{5,4},{6,5},{7,6},{9,8},{10,9},{11,10},{13,12},{... | collective-permute-start | bytes 18440 | tf_op jit(solution)/shard_map/ppermute | solution.py:371
  308.2 59.0 %collective-permute-start.11 = (bf16[2,256,768]{2,1,0:T(8,128)(2,1)}, bf16[2,256,768]{2,1,0:T(8,128)(2,1)}, u32[]{:S(2)}, u32[]{:S(2)}) collective-permute-start(bf16[2,256,768]{2,1,0:T(8,128)(2,1)} %get-tuple-element.128), channel_id=1, source_target_pairs={{0,16},{4,20},{8,24},{12,28},{16,0},{20,4},{24,8},{28,12},{1,17},{... | collective-permute-start | bytes 2359304 | tf_op jit(solution)/shard_map/ppermute | solution.py:338
  308.7 58.4 %collective-permute-start.10 = (bf16[2,256,768]{2,1,0:T(8,128)(2,1)}, bf16[2,256,768]{2,1,0:T(8,128)(2,1)}, u32[]{:S(2)}, u32[]{:S(2)}) collective-permute-start(bf16[2,256,768]{2,1,0:T(8,128)(2,1)} %get-tuple-element.126), channel_id=1, source_target_pairs={{0,8},{4,12},{8,0},{12,4},{16,24},{20,28},{24,16},{28,20},{1,9},{5... | collective-permute-start | bytes 2359304 | tf_op jit(solution)/shard_map/ppermute | solution.py:338
  330.1 188.5 %reduce-scatter.6.cloned.1.call-start = ((), (), s32[]{:S(2)}) async-start(), calls=%async_computation.9 | async-start | bytes 5308416 | tf_op jit(solution)/shard_map/reduce_scatter | solution.py:817
  369.5 23.6 %all-to-all-start.2 = ((bf16[4,2,256,192]{2,3,1,0:T(8,128)(2,1)}), bf16[4,2,256,192]{2,3,1,0:T(8,128)(2,1)S(1)}, u32[]{:S(2)}, u32[]{:S(2)}) async-start(bf16[4,2,256,192]{2,3,1,0:T(8,128)(2,1)} %copy.153), calls=%async_computation.3 | async-start | bytes 1572864 | tf_op jit(solution)/shard_map/all_to_all | solution.py:327
  431.7 48.2 %collective-permute-start.14 = (bf16[576,1536]{1,0:T(8,128)(2,1)}, bf16[576,1536]{1,0:T(8,128)(2,1)}, u32[]{:S(2)}, u32[]{:S(2)}) collective-permute-start(bf16[576,1536]{1,0:T(8,128)(2,1)} %reduce-scatter.4.cloned.1.call-done), channel_id=1, source_target_pairs={{0,1},{3,2},{4,5},{7,6},{8,9},{11,10},{12,13},{15,14},{16,17},{19,... | collective-permute-start | bytes 5308424 | tf_op jit(solution)/shard_map/ppermute | solution.py:381
  438.6 70.2 %all-to-all-start.3 = ((bf16[4,2,256,576]{2,3,1,0:T(8,128)(2,1)}), bf16[4,2,256,576]{2,3,1,0:T(8,128)(2,1)S(1)}, u32[]{:S(2)}, u32[]{:S(2)}) async-start(bf16[4,2,256,576]{2,3,1,0:T(8,128)(2,1)} %copy.157), calls=%async_computation.4 | async-start | bytes 4718592 | tf_op jit(solution)/shard_map/all_to_all | solution.py:327
  483.8 130.3 %collective-permute-start.17 = (bf16[576,1536]{1,0:T(8,128)(2,1)}, bf16[576,1536]{1,0:T(8,128)(2,1)}, u32[]{:S(2)}, u32[]{:S(2)}) collective-permute-start(bf16[576,1536]{1,0:T(8,128)(2,1)} %add.273), channel_id=1, source_target_pairs={{1,2},{2,1},{5,6},{6,5},{9,10},{10,9},{13,14},{14,13},{17,18},{18,... | collective-permute-start | bytes 5308424 | tf_op jit(solution)/shard_map/ppermute | solution.py:381
  616.5 40.9 %collective-permute-start.18 = (bf16[576,1536]{1,0:T(8,128)(2,1)S(1)}, bf16[576,1536]{1,0:T(8,128)(2,1)}, u32[]{:S(2)}, u32[]{:S(2)}) collective-permute-start(bf16[576,1536]{1,0:T(8,128)(2,1)S(1)} %add.276), channel_id=1, source_target_pairs={{1,0},{2,3},{5,4},{6,7},{9,8},{10,11},{13,12},{14,15},{17,16},{18,... | collective-permute-start | bytes 5308424 | tf_op jit(solution)/shard_map/ppermute | solution.py:388
  628.5 18.2 %collective-permute-start.15 = (bf16[2,256,768]{2,1,0:T(8,128)(2,1)}, bf16[2,256,768]{2,1,0:T(8,128)(2,1)}, u32[]{:S(2)}, u32[]{:S(2)}) collective-permute-start(bf16[2,256,768]{2,1,0:T(8,128)(2,1)} %broadcast_select_fusion.5), channel_id=1, source_target_pairs={{0,16},{4,20},{8,24},{12,28},{16,0},{20,4},{24,8},{28,12},{1,17},{... | collective-permute-start | bytes 2359304 | tf_op jit(solution)/shard_map/ppermute | solution.py:338
  629.7 17.7 %collective-permute-start.16 = (bf16[2,256,768]{2,1,0:T(8,128)(2,1)}, bf16[2,256,768]{2,1,0:T(8,128)(2,1)}, u32[]{:S(2)}, u32[]{:S(2)}) collective-permute-start(bf16[2,256,768]{2,1,0:T(8,128)(2,1)} %broadcast_select_fusion.9), channel_id=1, source_target_pairs={{0,8},{4,12},{8,0},{12,4},{16,24},{20,28},{24,16},{28,20},{1,9},{5... | collective-permute-start | bytes 2359304 | tf_op jit(solution)/shard_map/ppermute | solution.py:338
  (71 other events, 396.3 us)
Sparse Core Ops, SparseCore 0:
  14.1 60.1 all-gather.7
  76.2 90.9 all-gather.9
  169.1 86.8 all-gather.5
  294.3 100.8 reduce-scatter.3
  398.4 42.3 reduce-scatter.7
  444.1 53.7 reduce-scatter.5
